TPU v7x, 32 devices: a whole 2x2x4 slice. The times are simulated.
32 devices in a mesh: fsdp: 2 (over x), ctx: 4 (over y, core), tp: 4 (over z).
Axes of the slice: x: 2, y: 2, z: 4, core: 2. Of those that a mesh axis runs over, the one named last changes fastest.
Arguments:
- inputs: bfloat16 [16, 680, 1024], P('fsdp', 'ctx', 'tp'), may hold values from -6 to 6
- cotangent: bfloat16 [16, 680, 1024], P('fsdp', 'ctx', 'tp'), may hold values from -6 to 6
- labels: int32 [16], replicated, may hold values from 0 to 1000
- scale_ids: int32 [680], replicated, may hold values from 0 to 9, never falling along the last dimension, each value on 1 to 256 neighbouring positions
- head_flags: int32 [16], P('tp'), may hold values 0 or 1
- class_table: bfloat16 [1001, 1024], P(None, ('fsdp', 'ctx', 'tp')), may hold values from -6 to 6
- modulate_weight: bfloat16 [1024, 6, 1024], P(('fsdp', 'ctx'), None, 'tp'), may hold values from -0.1875 to 0.1875
- modulate_bias: bfloat16 [6, 16, 64], P(None, 'tp', ('fsdp', 'ctx')), may hold values from -3 to 3
- query_weight: bfloat16 [1024, 1024], P(('fsdp', 'ctx'), 'tp'), may hold values from -0.1875 to 0.1875
- key_weight: bfloat16 [1024, 1024], P(('fsdp', 'ctx'), 'tp'), may hold values from -0.1875 to 0.1875
- value_weight: bfloat16 [1024, 1024], P(('fsdp', 'ctx'), 'tp'), may hold values from -0.1875 to 0.1875
- query_bias: bfloat16 [16, 64], P('tp', ('fsdp', 'ctx')), may hold values from -3 to 3
- value_bias: bfloat16 [16, 64], P('tp', ('fsdp', 'ctx')), may hold values from -3 to 3
- query_gain: bfloat16 [16, 64], P('tp', ('fsdp', 'ctx')), may hold values from 0.69 to 2.27
- key_gain: bfloat16 [16, 64], P('tp', ('fsdp', 'ctx')), may hold values from 0.69 to 2.27
- output_weight: bfloat16 [1024, 1024], P('tp', ('fsdp', 'ctx')), may hold values from -1 to 1
- output_bias: bfloat16 [16, 64], P('tp', ('fsdp', 'ctx')), may hold values from -2 to 2
- up_weight: bfloat16 [1024, 4096], P(('fsdp', 'ctx'), 'tp'), may hold values from -0.1875 to 0.1875
- up_bias: bfloat16 [64, 64], P('tp', ('fsdp', 'ctx')), may hold values from -3 to 3
- down_weight: bfloat16 [4096, 1024], P('tp', ('fsdp', 'ctx')), may hold values from -0.09375 to 0.09375
- down_bias: bfloat16 [16, 64], P('tp', ('fsdp', 'ctx')), may hold values from -2 to 2
Outputs:
- block_out: bfloat16 [16, 680, 1024], P('fsdp', 'ctx', 'tp')
- inputs_grad: float32 [16, 680, 1024], P('fsdp', 'ctx', 'tp')
- class_table_grad: float32 [1001, 1024], P(None, ('fsdp', 'ctx', 'tp'))
- modulate_weight_grad: float32 [1024, 6, 1024], P(('fsdp', 'ctx'), None, 'tp')
- modulate_bias_grad: float32 [6, 16, 64], P(None, 'tp', ('fsdp', 'ctx'))
- query_weight_grad: float32 [1024, 1024], P(('fsdp', 'ctx'), 'tp')
- key_weight_grad: float32 [1024, 1024], P(('fsdp', 'ctx'), 'tp')
- value_weight_grad: float32 [1024, 1024], P(('fsdp', 'ctx'), 'tp')
- query_bias_grad: float32 [16, 64], P('tp', ('fsdp', 'ctx'))
- value_bias_grad: float32 [16, 64], P('tp', ('fsdp', 'ctx'))
- query_gain_grad: float32 [16, 64], P('tp', ('fsdp', 'ctx'))
- key_gain_grad: float32 [16, 64], P('tp', ('fsdp', 'ctx'))
- output_weight_grad: float32 [1024, 1024], P('tp', ('fsdp', 'ctx'))
- output_bias_grad: float32 [16, 64], P('tp', ('fsdp', 'ctx'))
- up_weight_grad: float32 [1024, 4096], P(('fsdp', 'ctx'), 'tp')
- up_bias_grad: float32 [64, 64], P('tp', ('fsdp', 'ctx'))
- down_weight_grad: float32 [4096, 1024], P('tp', ('fsdp', 'ctx'))
- down_bias_grad: float32 [16, 64], P('tp', ('fsdp', 'ctx'))
- clipped_query: float32 [1024, 1024], P(('fsdp', 'ctx'), 'tp')
- clipped_key: float32 [1024, 1024], P(('fsdp', 'ctx'), 'tp')
- clipped_query_bias: float32 [16, 64], P('tp', ('fsdp', 'ctx'))
Inputs may be any that keep to these rules, and one draw needn't show every extreme that they name: scale_ids never fall along a pyramid; each of the 10 scales holds 1 to 256 consecutive tokens and one holds exactly 256.
All inputs are finite; a program needn't handle non-finite values. No bound on the sum of `head_flags` on one device may be relied on, other than what follows from the above.
Results may differ from a plain program's by a relative error of at most 0.019.
Values may be sent and summed in bfloat16 or wider, within the bound.
A program may use at most 192 MiB of HBM per device.

v0:
```python
import math

import jax
import jax.numpy as jnp
from jax import lax
from jax.sharding import PartitionSpec as P

HD = 64


precise = lax.Precision.HIGHEST
norm_epsilon = 1e-06
clip_threshold = 2.0
masked_score = -1e30


def layer_norm(values):
    centered = values - jnp.mean(values, axis=-1, keepdims=True)
    spread = jnp.mean(centered * centered, axis=-1, keepdims=True)
    return centered * lax.rsqrt(spread + norm_epsilon)


def head_norm(values, gains):
    return (
        values * lax.rsqrt(jnp.mean(values * values, axis=-1, keepdims=True) + norm_epsilon) * gains
    )


def modulated(values, shift, scale):
    return layer_norm(values) * (1.0 + scale) + shift


def gelu_tanh(values):
    return jax.nn.gelu(values, approximate=True)


def product(left, right, form):
    return jnp.einsum(form, left, right, preferred_element_type=jnp.float32)


def whole_rows(values, shifts):
    return (
        lax.all_gather(values, "tp", axis=2, tiled=True),
        lax.all_gather(shifts, "tp", axis=2, tiled=True),
    )


def branch_sum(partial_rows):
    return lax.psum_scatter(
        partial_rows.astype(jnp.bfloat16), "tp", scatter_dimension=2, tiled=True
    ).astype(jnp.float32)


def whole_grad(values):
    return lax.all_gather(values, "tp", axis=2, tiled=True)


def row_grads(partial_rows, partial_mods):
    return (
        lax.psum_scatter(
            partial_rows.astype(jnp.bfloat16), "tp", scatter_dimension=2, tiled=True
        ).astype(jnp.float32),
        lax.psum_scatter(
            partial_mods.astype(jnp.bfloat16), "tp", scatter_dimension=2, tiled=True
        ).astype(jnp.float32),
    )


def norm_backward(rows, shift, scale, incoming):
    primal, pullback = jax.vjp(modulated, rows, shift, scale)
    return pullback(incoming)


def scores_of(query_block, key_block):
    return jnp.einsum(
        "qhd,khd->hqk", query_block, key_block, preferred_element_type=jnp.float32
    ) / math.sqrt(HD)


def forward_scan(allowed, query_blocks, key_blocks, value_blocks):

    def attend_image(state, blocks):
        query_block, key_block, value_block = blocks
        scores = scores_of(query_block, key_block)
        highest = jnp.max(jnp.where(allowed, scores, -jnp.inf), axis=(1, 2))
        masked = jnp.where(allowed, scores, masked_score)
        row_peak = jnp.max(masked, axis=-1, keepdims=True)
        log_total = row_peak + jnp.log(jnp.sum(jnp.exp(masked - row_peak), axis=-1, keepdims=True))
        probs = jnp.exp(masked - log_total).astype(jnp.bfloat16)
        attended = jnp.einsum(
            "hqk,khd->qhd", probs, value_block, preferred_element_type=jnp.float32
        )
        return (state, (attended, log_total, highest))

    unused, results = lax.scan(attend_image, jnp.int32(0), (query_blocks, key_blocks, value_blocks))
    return results


def backward_scan(allowed, query_blocks, key_blocks, value_blocks, log_totals, delta_blocks):

    def attend_back(state, blocks):
        query_block, key_block, value_block, log_total, delta_block = blocks
        scores = scores_of(query_block, key_block)
        probs = jnp.exp(jnp.where(allowed, scores, masked_score) - log_total)
        prob_delta = jnp.einsum(
            "qhd,khd->hqk", delta_block, value_block, preferred_element_type=jnp.float32
        )
        centre = jnp.sum(probs * prob_delta, axis=-1, keepdims=True)
        score_delta = (probs * (prob_delta - centre)).astype(jnp.bfloat16)
        query_part = jnp.einsum(
            "hqk,khd->qhd", score_delta, key_block, preferred_element_type=jnp.float32
        ) / math.sqrt(HD)
        key_part = jnp.einsum(
            "hqk,qhd->khd", score_delta, query_block, preferred_element_type=jnp.float32
        ) / math.sqrt(HD)
        value_part = jnp.einsum(
            "hqk,qhd->khd",
            probs.astype(jnp.bfloat16),
            delta_block,
            preferred_element_type=jnp.float32,
        )
        return (state, (query_part, key_part, value_part))

    unused, results = lax.scan(
        attend_back,
        jnp.int32(0),
        (query_blocks, key_blocks, value_blocks, log_totals, delta_blocks),
    )
    return results


def on_device(
    inputs,
    cotangent,
    labels,
    scale_ids,
    head_flags,
    class_table,
    modulate_weight,
    modulate_bias,
    query_weight,
    key_weight,
    value_weight,
    query_bias,
    value_bias,
    query_gain,
    key_gain,
    output_weight,
    output_bias,
    up_weight,
    up_bias,
    down_weight,
    down_bias,
):
    images, rows_here, local_width = inputs.shape
    length = scale_ids.shape[0]
    first_image = lax.axis_index("fsdp") * images
    first_row = lax.axis_index("ctx") * rows_here
    classes = class_table.shape[0]
    onehot = (labels[:, None] == jnp.arange(classes, dtype=jnp.int32)[None, :]).astype(jnp.bfloat16)
    cond_part = jnp.dot(onehot, class_table, preferred_element_type=jnp.float32).astype(
        jnp.bfloat16
    )
    cond_every = lax.all_gather(cond_part, ("fsdp", "ctx", "tp"), axis=1, tiled=True)
    condition = lax.dynamic_slice_in_dim(cond_every, first_image, images, 0).astype(jnp.float32)
    gathered = (
        lax.all_gather(modulate_weight, ("fsdp", "ctx"), axis=0, tiled=True),
        lax.all_gather(query_weight, ("fsdp", "ctx"), axis=0, tiled=True),
        lax.all_gather(key_weight, ("fsdp", "ctx"), axis=0, tiled=True),
        lax.all_gather(value_weight, ("fsdp", "ctx"), axis=0, tiled=True),
        lax.all_gather(output_weight, ("fsdp", "ctx"), axis=1, tiled=True),
        lax.all_gather(up_weight, ("fsdp", "ctx"), axis=0, tiled=True),
        lax.all_gather(down_weight, ("fsdp", "ctx"), axis=1, tiled=True),
        lax.all_gather(modulate_bias, ("fsdp", "ctx"), axis=2, tiled=True),
        lax.all_gather(query_bias, ("fsdp", "ctx"), axis=1, tiled=True),
        lax.all_gather(value_bias, ("fsdp", "ctx"), axis=1, tiled=True),
        lax.all_gather(query_gain, ("fsdp", "ctx"), axis=1, tiled=True),
        lax.all_gather(key_gain, ("fsdp", "ctx"), axis=1, tiled=True),
        lax.all_gather(output_bias, ("fsdp", "ctx"), axis=1, tiled=True),
        lax.all_gather(up_bias, ("fsdp", "ctx"), axis=1, tiled=True),
        lax.all_gather(down_bias, ("fsdp", "ctx"), axis=1, tiled=True),
    )
    (
        modulate_full,
        query_full,
        key_full,
        value_full,
        output_full,
        up_full,
        down_full,
        modulate_shift,
        query_shift,
        value_shift,
        query_gains,
        key_gains,
        output_shift,
        up_shift,
        down_shift,
    ) = gathered
    heads_here = query_gains.shape[0]
    silu_cond = jax.nn.silu(condition).astype(jnp.bfloat16)
    modulation = (
        product(silu_cond, modulate_full, "bd,dje->bje")
        + modulate_shift.reshape(6, local_width).astype(jnp.float32)
    ).astype(jnp.bfloat16)
    inputs_full, shift_scale_one = whole_rows(inputs, modulation[:, 0:2])
    inputs_wide = inputs_full.astype(jnp.float32)
    shift_one = shift_scale_one[:, 0:1].astype(jnp.float32)
    scale_one = shift_scale_one[:, 1:2].astype(jnp.float32)
    normed_one = modulated(inputs_wide, shift_one, scale_one).astype(jnp.bfloat16)
    query_pre = product(normed_one, query_full, "bsd,de->bse") + query_shift.reshape(-1).astype(
        jnp.float32
    )
    key_pre = product(normed_one, key_full, "bsd,de->bse")
    value_rows = (
        product(normed_one, value_full, "bsd,de->bse") + value_shift.reshape(-1).astype(jnp.float32)
    ).astype(jnp.bfloat16)
    query_heads = query_pre.reshape(images, rows_here, heads_here, HD)
    key_heads = key_pre.reshape(images, rows_here, heads_here, HD)
    query_hat = head_norm(query_heads, query_gains.astype(jnp.float32)).astype(jnp.bfloat16)
    key_hat = head_norm(key_heads, key_gains.astype(jnp.float32)).astype(jnp.bfloat16)
    key_flat = key_hat.reshape(images, rows_here, local_width)
    query_ids = lax.dynamic_slice_in_dim(scale_ids, first_row, rows_here, 0)
    row_allowed = (scale_ids[None, :] <= query_ids[:, None])[None]
    keys_every, values_every = (
        lax.all_gather(key_flat, "ctx", axis=1, tiled=True),
        lax.all_gather(value_rows, "ctx", axis=1, tiled=True),
    )
    key_blocks = keys_every.reshape(images, length, heads_here, HD)
    value_blocks = values_every.reshape(images, length, heads_here, HD)
    attended, log_totals, highest = forward_scan(row_allowed, query_hat, key_blocks, value_blocks)
    attended_low = attended.reshape(images, rows_here, local_width).astype(jnp.bfloat16)
    head_max = lax.pmax(jnp.max(highest, axis=0), ("fsdp", "ctx"))
    branch_one = branch_sum(
        product(attended_low, output_full, "bse,ef->bsf")
    ) + output_shift.reshape(-1).astype(jnp.float32)
    gate_one = modulation[:, 2:3].astype(jnp.float32)
    middle = (inputs.astype(jnp.float32) + gate_one * branch_one).astype(jnp.bfloat16)
    middle_full, shift_scale_two = whole_rows(middle, modulation[:, 3:5])
    middle_wide = middle_full.astype(jnp.float32)
    shift_two = shift_scale_two[:, 0:1].astype(jnp.float32)
    scale_two = shift_scale_two[:, 1:2].astype(jnp.float32)
    normed_two = modulated(middle_wide, shift_two, scale_two).astype(jnp.bfloat16)
    hidden_pre = product(normed_two, up_full, "bsd,dh->bsh") + up_shift.reshape(-1).astype(
        jnp.float32
    )
    hidden = gelu_tanh(hidden_pre).astype(jnp.bfloat16)
    branch_two = branch_sum(product(hidden, down_full, "bsh,hf->bsf")) + down_shift.reshape(
        -1
    ).astype(jnp.float32)
    gate_two = modulation[:, 5:6].astype(jnp.float32)
    block_out = (middle.astype(jnp.float32) + gate_two * branch_two).astype(jnp.bfloat16)
    factor = jnp.where(
        head_flags == 1,
        jnp.sqrt(clip_threshold / jnp.maximum(head_max, clip_threshold)),
        jnp.ones_like(head_max),
    )
    columns = jnp.repeat(factor, HD)
    clipped_query = query_weight.astype(jnp.float32) * columns[None, :]
    clipped_key = key_weight.astype(jnp.float32) * columns[None, :]
    clipped_query_bias = query_bias.astype(jnp.float32) * factor[:, None]
    incoming = cotangent.astype(jnp.float32)
    down_delta = (incoming * gate_two).astype(jnp.bfloat16)
    gate_two_delta = jnp.sum(incoming * branch_two, axis=1)
    down_bias_part = jnp.sum(down_delta.astype(jnp.float32), axis=(0, 1)).reshape(heads_here, HD)
    down_delta_full = whole_grad(down_delta)
    down_weight_part = product(hidden, down_delta_full, "bsh,bsf->hf")
    hidden_delta = product(down_delta_full, down_full, "bsf,hf->bsh")
    primal, gelu_back = jax.vjp(gelu_tanh, hidden_pre)
    pre_delta = gelu_back(hidden_delta)[0].astype(jnp.bfloat16)
    up_bias_part = jnp.sum(pre_delta.astype(jnp.float32), axis=(0, 1)).reshape(-1, HD)
    up_weight_part = product(normed_two, pre_delta, "bsd,bsh->dh")
    normed_two_delta = product(pre_delta, up_full, "bsh,dh->bsd")
    middle_part, shift_two_delta, scale_two_delta = norm_backward(
        middle_wide, shift_two, scale_two, normed_two_delta
    )
    middle_delta, two_deltas = row_grads(
        middle_part, jnp.concatenate([shift_two_delta, scale_two_delta], axis=1)
    )
    middle_delta = middle_delta + incoming
    branch_delta = (middle_delta * gate_one).astype(jnp.bfloat16)
    gate_one_delta = jnp.sum(middle_delta * branch_one, axis=1)
    output_bias_part = jnp.sum(branch_delta.astype(jnp.float32), axis=(0, 1)).reshape(
        heads_here, HD
    )
    branch_delta_full = whole_grad(branch_delta)
    output_weight_part = product(attended_low, branch_delta_full, "bse,bsf->ef")
    attended_delta = product(branch_delta_full, output_full, "bsf,ef->bse").astype(jnp.bfloat16)
    delta_heads = attended_delta.reshape(images, rows_here, heads_here, HD)
    query_hat_delta, key_parts, value_parts = backward_scan(
        row_allowed, query_hat, key_blocks, value_blocks, log_totals, delta_heads
    )
    key_hat_delta, values_delta = (
        lax.psum_scatter(
            key_parts.reshape(images, length, local_width).astype(jnp.bfloat16),
            "ctx",
            scatter_dimension=1,
            tiled=True,
        ).astype(jnp.float32),
        lax.psum_scatter(
            value_parts.reshape(images, length, local_width).astype(jnp.bfloat16),
            "ctx",
            scatter_dimension=1,
            tiled=True,
        ).astype(jnp.float32),
    )
    values_low = values_delta.astype(jnp.bfloat16)
    primal, query_norm_back = jax.vjp(head_norm, query_heads, query_gains.astype(jnp.float32))
    query_delta_heads, query_gain_part = query_norm_back(query_hat_delta)
    primal, key_norm_back = jax.vjp(head_norm, key_heads, key_gains.astype(jnp.float32))
    key_delta_heads, key_gain_part = key_norm_back(
        key_hat_delta.reshape(images, rows_here, heads_here, HD)
    )
    queries_delta = query_delta_heads.reshape(images, rows_here, local_width).astype(jnp.bfloat16)
    keys_delta = key_delta_heads.reshape(images, rows_here, local_width).astype(jnp.bfloat16)
    query_bias_part = jnp.sum(queries_delta.astype(jnp.float32), axis=(0, 1)).reshape(
        heads_here, HD
    )
    value_bias_part = jnp.sum(values_low.astype(jnp.float32), axis=(0, 1)).reshape(heads_here, HD)
    query_weight_part = product(normed_one, queries_delta, "bsd,bse->de")
    key_weight_part = product(normed_one, keys_delta, "bsd,bse->de")
    value_weight_part = product(normed_one, values_low, "bsd,bse->de")
    normed_one_delta = (
        product(queries_delta, query_full, "bse,de->bsd")
        + product(keys_delta, key_full, "bse,de->bsd")
        + product(values_low, value_full, "bse,de->bsd")
    )
    inputs_part, shift_one_delta, scale_one_delta = norm_backward(
        inputs_wide, shift_one, scale_one, normed_one_delta
    )
    inputs_delta, one_deltas = row_grads(
        inputs_part, jnp.concatenate([shift_one_delta, scale_one_delta], axis=1)
    )
    inputs_grad = middle_delta + inputs_delta
    modulation_delta = jnp.concatenate(
        [one_deltas, gate_one_delta[:, None], two_deltas, gate_two_delta[:, None]], axis=1
    )
    modulate_bias_part = jnp.sum(modulation_delta, axis=0).reshape(6, heads_here, HD)
    modulate_weight_part = jnp.einsum(
        "bd,bje->dje", silu_cond.astype(jnp.float32), modulation_delta, precision=precise
    )
    silu_delta = jnp.einsum(
        "bje,dje->bd", modulation_delta, modulate_full.astype(jnp.float32), precision=precise
    )
    primal, silu_back = jax.vjp(jax.nn.silu, condition)
    cond_delta = silu_back(silu_delta)[0]
    every_delta = lax.dynamic_update_slice_in_dim(
        jnp.zeros((cond_every.shape[0], cond_every.shape[1]), jnp.float32),
        cond_delta,
        first_image,
        0,
    )
    cond_cols_delta = lax.psum_scatter(
        every_delta, ("fsdp", "ctx", "tp"), scatter_dimension=1, tiled=True
    )
    class_table_grad = jnp.dot(onehot.astype(jnp.float32).T, cond_cols_delta, precision=precise)
    summed = (
        lax.psum_scatter(modulate_weight_part, ("fsdp", "ctx"), scatter_dimension=0, tiled=True),
        lax.psum_scatter(query_weight_part, ("fsdp", "ctx"), scatter_dimension=0, tiled=True),
        lax.psum_scatter(key_weight_part, ("fsdp", "ctx"), scatter_dimension=0, tiled=True),
        lax.psum_scatter(value_weight_part, ("fsdp", "ctx"), scatter_dimension=0, tiled=True),
        lax.psum_scatter(output_weight_part, ("fsdp", "ctx"), scatter_dimension=1, tiled=True),
        lax.psum_scatter(up_weight_part, ("fsdp", "ctx"), scatter_dimension=0, tiled=True),
        lax.psum_scatter(down_weight_part, ("fsdp", "ctx"), scatter_dimension=1, tiled=True),
        lax.psum_scatter(modulate_bias_part, ("fsdp", "ctx"), scatter_dimension=2, tiled=True),
        lax.psum_scatter(query_bias_part, ("fsdp", "ctx"), scatter_dimension=1, tiled=True),
        lax.psum_scatter(value_bias_part, ("fsdp", "ctx"), scatter_dimension=1, tiled=True),
        lax.psum_scatter(query_gain_part, ("fsdp", "ctx"), scatter_dimension=1, tiled=True),
        lax.psum_scatter(key_gain_part, ("fsdp", "ctx"), scatter_dimension=1, tiled=True),
        lax.psum_scatter(output_bias_part, ("fsdp", "ctx"), scatter_dimension=1, tiled=True),
        lax.psum_scatter(up_bias_part, ("fsdp", "ctx"), scatter_dimension=1, tiled=True),
        lax.psum_scatter(down_bias_part, ("fsdp", "ctx"), scatter_dimension=1, tiled=True),
    )
    return (
        block_out,
        inputs_grad,
        class_table_grad,
        summed[0],
        summed[7],
        summed[1],
        summed[2],
        summed[3],
        summed[8],
        summed[9],
        summed[10],
        summed[11],
        summed[4],
        summed[12],
        summed[5],
        summed[13],
        summed[6],
        summed[14],
        clipped_query,
        clipped_key,
        clipped_query_bias,
    )


def solution(mesh):
    return jax.shard_map(
        on_device,
        mesh=mesh,
        in_specs=(
            P("fsdp", "ctx", "tp"),
            P("fsdp", "ctx", "tp"),
            P(),
            P(),
            P("tp"),
            P(None, ("fsdp", "ctx", "tp")),
            P(("fsdp", "ctx"), None, "tp"),
            P(None, "tp", ("fsdp", "ctx")),
            P(("fsdp", "ctx"), "tp"),
            P(("fsdp", "ctx"), "tp"),
            P(("fsdp", "ctx"), "tp"),
            P("tp", ("fsdp", "ctx")),
            P("tp", ("fsdp", "ctx")),
            P("tp", ("fsdp", "ctx")),
            P("tp", ("fsdp", "ctx")),
            P("tp", ("fsdp", "ctx")),
            P("tp", ("fsdp", "ctx")),
            P(("fsdp", "ctx"), "tp"),
            P("tp", ("fsdp", "ctx")),
            P("tp", ("fsdp", "ctx")),
            P("tp", ("fsdp", "ctx")),
        ),
        out_specs=(
            P("fsdp", "ctx", "tp"),
            P("fsdp", "ctx", "tp"),
            P(None, ("fsdp", "ctx", "tp")),
            P(("fsdp", "ctx"), None, "tp"),
            P(None, "tp", ("fsdp", "ctx")),
            P(("fsdp", "ctx"), "tp"),
            P(("fsdp", "ctx"), "tp"),
            P(("fsdp", "ctx"), "tp"),
            P("tp", ("fsdp", "ctx")),
            P("tp", ("fsdp", "ctx")),
            P("tp", ("fsdp", "ctx")),
            P("tp", ("fsdp", "ctx")),
            P("tp", ("fsdp", "ctx")),
            P("tp", ("fsdp", "ctx")),
            P(("fsdp", "ctx"), "tp"),
            P("tp", ("fsdp", "ctx")),
            P("tp", ("fsdp", "ctx")),
            P("tp", ("fsdp", "ctx")),
            P(("fsdp", "ctx"), "tp"),
            P(("fsdp", "ctx"), "tp"),
            P("tp", ("fsdp", "ctx")),
        ),
        check_vma=False,
    )
```

profile of v0, /device:TPU:0, one launch (start us, length us, event | category | flops | bytes accessed | tf_op | source)
XLA Modules:
  0.0 1448.9 jit_solution(10858788953981037282)
XLA Ops:
  11.1 76.0 %all-gather = bf16[32,32,16]{1,2,0:T(8,128)(2,1)S(1)} all-gather(bf16[1,32,16]{1,2,0:T(8,128)(2,1)S(1)} %fusion.91), channel_id=1, replica_groups=mesh['fsdp'=2,'ctx'=4,'tp'=4] {'fsdp','ctx','tp'}, dimensions={0}, use_global_device_ids=true | all-gather | bytes 33792 | tf_op jit(solution)/shard_map/all_gather | solution.py:164
  87.4 12.8 all_gather.74
  100.4 7.7 all-gather.4
  108.3 10.1 all_gather.83
  124.6 13.1 all_gather.76
  153.5 7.7 all-gather.1
  161.4 12.6 all_gather.77
  176.7 7.8 all-gather.2
  184.6 9.0 all-gather.3
  193.8 11.2 all_gather.80
  205.1 11.3 all_gather.86
  222.3 4.9 copy.214
  232.2 53.2 %while.32 = (s32[]{:T(128)}, bf16[8,170,4,64]{1,3,2,0:T(8,128)(2,1)}, f32[8,4,170,1]{2,1,3,0:T(4,128)S(1)}, f32[8,4]{1,0:T(8,128)}, bf16[8,680,4,64]{1,3,2,0:T(8...) while((s32[]{:T(128)}, ...), condition=%wide.region_8.9_spmd.clone.clone, body=%wide.region_4.8_spmd.clone.sunk.clone | while | flops 124500512 | bytes 7243277 | solution.py:95
  289.4 8.0 all-gather.5
  297.5 47.8 %reduce-scatter.27.cloned.1.call-done = bf16[8,170,256]{2,1,0:T(8,128)(2,1)} async-done(((bf16[8,170,1024]{2,1,0:T(8,128)(2,1)}), bf16[8,170,256]{2,1,0:T(8,128)(2,1)}) %reduce-scatter.27.cloned.1.call-update) | async-done | bytes 696336 | tf_op jit(solution)/shard_map/reduce_scatter | solution.py:49
  351.6 8.9 all_gather.91
  360.6 15.4 %all_gather.89 = bf16[8,2,1024]{2,0,1:T(8,128)(2,1)S(1)} all-gather(bf16[8,2,256]{2,0,1:T(8,128)(2,1)S(1)} %get-tuple-element.399), channel_id=1, replica_groups=mesh['fsdp'=2,'ctx'=4,'tp'=4] {'tp'}, dimensions={2}, use_global_device_ids=true | all-gather | bytes 40960 | tf_op jit(solution)/shard_map/all_gather | solution.py:44
  376.1 31.4 %all-gather.25.cloned.1.call-done = bf16[8,170,1024]{2,1,0:T(8,128)(2,1)} async-done(((bf16[8,170,256]{2,1,0:T(8,128)(2,1)}), bf16[8,170,1024]{2,1,0:T(8,128)(2,1)}) %all-gather.25.cloned.1.call-update) | async-done | bytes 2785296 | tf_op jit(solution)/shard_map/all_gather | solution.py:43
  411.1 24.4 %all-gather.27.cloned.1.call-done = bf16[1024,1024]{1,0:T(8,128)(2,1)} async-done(((bf16[128,1024]{1,0:T(8,128)(2,1)}), bf16[1024,1024]{1,0:T(8,128)(2,1)}) %all-gather.27.cloned.1.call-update) | async-done | bytes 2097168 | tf_op jit(solution)/shard_map/all_gather | solution.py:172
  435.5 8.3 fusion.82
  443.8 21.8 %all-gather.29.cloned.1.call-done = bf16[1024,1024]{1,0:T(8,128)(2,1)} async-done(((bf16[1024,128]{1,0:T(8,128)(2,1)}), bf16[1024,1024]{1,0:T(8,128)(2,1)}) %all-gather.29.cloned.1.call-update) | async-done | bytes 2097168 | tf_op jit(solution)/shard_map/all_gather | solution.py:173
  465.6 60.7 %all-gather.31.cloned.1.call-done = bf16[8,170,1024]{2,1,0:T(8,128)(2,1)} async-done(((bf16[8,170,256]{2,1,0:T(8,128)(2,1)}), bf16[8,170,1024]{2,1,0:T(8,128)(2,1)}) %all-gather.31.cloned.1.call-update) | async-done | bytes 2785296 | tf_op jit(solution)/shard_map/all_gather | solution.py:55
  526.4 11.1 convert_reduce_fusion.2
  547.9 8.8 convolution_convert_fusion
  556.8 8.9 all-gather.6
  565.8 36.1 %reduce-scatter.31.cloned.1.call-done = bf16[8,170,256]{2,1,0:T(8,128)(2,1)} async-done(((bf16[8,170,1024]{2,1,0:T(8,128)(2,1)}), bf16[8,170,256]{2,1,0:T(8,128)(2,1)}) %reduce-scatter.31.cloned.1.call-update) | async-done | bytes 696336 | tf_op jit(solution)/shard_map/reduce_scatter | solution.py:60
  602.0 58.4 %reduce-scatter.29.cloned.1.call-done = bf16[8,170,256]{2,1,0:T(8,128)(2,1)} async-done(((bf16[8,170,1024]{2,1,0:T(8,128)(2,1)}), bf16[8,170,256]{2,1,0:T(8,128)(2,1)}) %reduce-scatter.29.cloned.1.call-update) | async-done | bytes 696336 | tf_op jit(solution)/shard_map/reduce_scatter | solution.py:49
  665.8 58.3 %all-gather.33.cloned.1.call-done = bf16[8,170,1024]{2,1,0:T(8,128)(2,1)} async-done(((bf16[8,170,256]{2,1,0:T(8,128)(2,1)}), bf16[8,170,1024]{2,1,0:T(8,128)(2,1)}) %all-gather.33.cloned.1.call-update) | async-done | bytes 2785296 | tf_op jit(solution)/shard_map/all_gather | solution.py:55
  730.0 74.1 %while.33 = (s32[]{:T(128)}, f32[8,170,4,64]{1,3,2,0:T(8,128)}, bf16[8,680,4,64]{1,3,2,0:T(8,128)(2,1)}, bf16[8,680,4,64]{1,3,2,0:T(8,128)(2,1)}, bf16[8,680,4,6...) while((s32[]{:T(128)}, f32[8,170,4,64]{1,3,2,0:T(8,128)}, ...), condition=%wide.region_18.19_spmd.clone.clone, body=%wide.region_16.18_spmd.clone.sunk.clone | while | flops 300430112 | bytes 18154952 | solution.py:124
  804.1 5.1 copy.222
  809.2 5.1 copy.227
  819.7 23.6 %reduce-scatter.33.cloned.1.call-done = bf16[8,170,256]{2,0,1:T(8,128)(2,1)} async-done(((bf16[8,680,256]{2,0,1:T(8,128)(2,1)}), bf16[8,170,256]{2,0,1:T(8,128)(2,1)}) %reduce-scatter.33.cloned.1.call-update) | async-done | bytes 696336 | tf_op jit(solution)/shard_map/reduce_scatter | solution.py:294
  862.2 19.1 %reduce-scatter.35.cloned.1.call-done = bf16[8,170,256]{2,0,1:T(8,128)(2,1)} async-done(((bf16[8,680,256]{2,0,1:T(8,128)(2,1)}), bf16[8,170,256]{2,0,1:T(8,128)(2,1)}) %reduce-scatter.35.cloned.1.call-update) | async-done | bytes 696336 | tf_op jit(solution)/shard_map/reduce_scatter | solution.py:300
  892.2 19.0 %reduce-scatter.39.cloned.1.call-done = bf16[8,2,256]{2,0,1:T(8,128)(2,1)} async-done(((bf16[8,2,1024]{2,0,1:T(8,128)(2,1)}), bf16[8,2,256]{2,0,1:T(8,128)(2,1)}) %reduce-scatter.39.cloned.1.call-update) | async-done | bytes 8208 | tf_op jit(solution)/shard_map/reduce_scatter | solution.py:63
  917.5 5.0 add_convert_fusion
  922.7 8.4 convolution_bitcast_fusion.3
  931.8 9.9 convolution_bitcast_fusion.2
  965.5 12.2 pmax.7
  982.4 23.2 %all-reduce.8 = (f32[6,4,64]{2,1,0:T(4,128)S(1)}, f32[4,64]{1,0:T(4,128)S(1)}, f32[4,64]{1,0:T(4,128)S(1)}, f32[4,64]{1,0:T(4,128)S(1)}, f32[4,64]{1,0:T(4,128)S...) all-reduce(f32[6,4,64]{2,1,0:T(4,128)S(1)} %reshape.332, ...), channel_id=12, replica_groups=mesh['fsdp'=2,'ctx'=4,'tp'=4] {'fsdp','ctx'}, use_global_device_ids=true, to_apply=%region_37.38.clone | all-reduce | flops 4096 | bytes 32768
  1009.0 41.2 %reduce-scatter.57.cloned.1.call-done = f32[32,16]{1,0:T(8,128)} async-done(((f32[1024,16]{1,0:T(8,128)}), f32[32,16]{1,0:T(8,128)}) %reduce-scatter.57.cloned.1.call-update) | async-done | bytes 2064
  1051.8 52.9 %reduce-scatter.37.cloned.1.call-done = bf16[8,170,256]{2,1,0:T(8,128)(2,1)} async-done(((bf16[8,170,1024]{2,1,0:T(8,128)(2,1)}), bf16[8,170,256]{2,1,0:T(8,128)(2,1)}) %reduce-scatter.37.cloned.1.call-update) | async-done | bytes 696336 | tf_op jit(solution)/shard_map/reduce_scatter | solution.py:60
  1108.0 52.3 %reduce-scatter.53.cloned.1.call-done = f32[128,1024]{1,0:T(8,128)} async-done(((f32[1024,1024]{1,0:T(8,128)}), f32[128,1024]{1,0:T(8,128)}) %reduce-scatter.53.cloned.1.call-update) | async-done | bytes 524304 | tf_op jit(solution)/shard_map/reduce_scatter | solution.py:363
  1160.2 55.1 %reduce-scatter.55.cloned.1.call-done = f32[1024,128]{1,0:T(8,128)} async-done(((f32[1024,1024]{1,0:T(8,128)}), f32[1024,128]{1,0:T(8,128)}) %reduce-scatter.55.cloned.1.call-update) | async-done | bytes 524304 | tf_op jit(solution)/shard_map/reduce_scatter | solution.py:364
  1215.4 40.2 %reduce-scatter.45.cloned.1.call-done = f32[128,256]{1,0:T(8,128)} async-done(((f32[1024,256]{1,0:T(8,128)}), f32[128,256]{1,0:T(8,128)}) %reduce-scatter.45.cloned.1.call-update) | async-done | bytes 131088 | tf_op jit(solution)/shard_map/reduce_scatter | solution.py:359
  1255.5 40.1 %reduce-scatter.51.cloned.1.call-done = f32[256,128]{1,0:T(8,128)} async-done(((f32[256,1024]{1,0:T(8,128)}), f32[256,128]{1,0:T(8,128)}) %reduce-scatter.51.cloned.1.call-update) | async-done | bytes 131088 | tf_op jit(solution)/shard_map/reduce_scatter | solution.py:362
  1295.7 40.1 %reduce-scatter.47.cloned.1.call-done = f32[128,256]{1,0:T(8,128)} async-done(((f32[1024,256]{1,0:T(8,128)}), f32[128,256]{1,0:T(8,128)}) %reduce-scatter.47.cloned.1.call-update) | async-done | bytes 131088 | tf_op jit(solution)/shard_map/reduce_scatter | solution.py:360
  1335.8 40.0 %reduce-scatter.49.cloned.1.call-done = f32[128,256]{1,0:T(8,128)} async-done(((f32[1024,256]{1,0:T(8,128)}), f32[128,256]{1,0:T(8,128)}) %reduce-scatter.49.cloned.1.call-update) | async-done | bytes 131088 | tf_op jit(solution)/shard_map/reduce_scatter | solution.py:361
  1375.8 66.1 %reduce-scatter.43.cloned.1.call-done = f32[128,6,256]{2,0,1:T(8,128)} async-done(((f32[1024,6,256]{2,0,1:T(8,128)}), f32[128,6,256]{2,0,1:T(8,128)}) %reduce-scatter.43.cloned.1.call-update) | async-done | bytes 786448 | tf_op jit(solution)/shard_map/reduce_scatter | solution.py:358
  (410 shorter events, 281.5 us)
Async XLA Ops:
  7.2 80.1 %copy-start.37 = (bf16[6,4,8]{2,1,0:T(4,128)(2,1)S(1)}, bf16[6,4,8]{2,1,0:T(4,128)(2,1)}, u32[]{:S(2)}) copy-start(bf16[6,4,8]{2,1,0:T(4,128)(2,1)} %param.32) | copy-start | bytes 1156
  7.2 93.2 %copy-start.47 = (bf16[4,8]{1,0:T(4,128)(2,1)S(1)}, bf16[4,8]{1,0:T(4,128)(2,1)}, u32[]{:S(2)}) copy-start(bf16[4,8]{1,0:T(4,128)(2,1)} %param.39) | copy-start | bytes 196
  7.2 101.0 %copy-start.23 = (bf16[128,256]{1,0:T(8,128)(2,1)S(1)}, bf16[128,256]{1,0:T(8,128)(2,1)}, u32[]{:S(2)}) copy-start(bf16[128,256]{1,0:T(8,128)(2,1)} %param.34) | copy-start | bytes 196612
  7.2 111.1 %all-gather.19.cloned.1.call-start = ((), (), s32[]{:S(2)}) async-start(), calls=%async_computation.17 | async-start | bytes 3604480 | tf_op jit(solution)/shard_map/all_gather | solution.py:43
  9.4 112.7 %all-gather.17.cloned.1.call-start = ((), (), s32[]{:S(2)}) async-start(), calls=%async_computation.16 | async-start | bytes 3538944 | tf_op jit(solution)/shard_map/all_gather | solution.py:167
  10.2 212.1 %all-gather.23.cloned.1.call-start = ((), (), s32[]{:S(2)}) async-start(), calls=%async_computation.19 | async-start | bytes 3481600 | tf_op jit(solution)/shard_map/all_gather | solution.py:226
  87.3 34.9 %copy-start.27 = (bf16[1024,16]{0,1:T(8,128)(2,1)}, bf16[1024,16]{0,1:T(8,128)(2,1)S(1)}, u32[]{:S(2)}) copy-start(bf16[1024,16]{0,1:T(8,128)(2,1)S(1)} %reshape.348) | copy-start | bytes 98308
  118.3 19.5 %copy-start.19 = (bf16[1024,256]{1,0:T(8,128)(2,1)}, bf16[1024,256]{1,0:T(8,128)(2,1)S(1)}, u32[]{:S(2)}) copy-start(bf16[1024,256]{1,0:T(8,128)(2,1)S(1)} %all_gather.83) | copy-start | bytes 1572868
  137.8 79.7 %copy-start.33 = (f32[8,1024]{1,0:T(8,128)}, f32[8,1024]{1,0:T(8,128)S(1)}, u32[]{:S(2)}) copy-start(f32[8,1024]{1,0:T(8,128)S(1)} %fusion.119) | copy-start | bytes 98308
  153.4 73.8 %all-gather.21.cloned.1.call-start = ((), (), s32[]{:S(2)}) async-start(), calls=%async_computation.18 | async-start | bytes 3481600 | tf_op jit(solution)/shard_map/all_gather | solution.py:227
  173.9 19.8 %copy-start.22 = (s32[680]{0:T(1024)S(1)}, s32[680]{0:T(1024)}, u32[]{:S(2)}) copy-start(s32[680]{0:T(1024)} %param.28) | copy-start | bytes 8164
  173.9 19.9 %copy-start.25 = (bf16[128,256]{1,0:T(8,128)(2,1)S(1)}, bf16[128,256]{1,0:T(8,128)(2,1)}, u32[]{:S(2)}) copy-start(bf16[128,256]{1,0:T(8,128)(2,1)} %param.33) | copy-start | bytes 196612
  173.9 31.1 %copy-start.32 = (bf16[256,128]{1,0:T(8,128)(2,1)S(1)}, bf16[256,128]{1,0:T(8,128)(2,1)}, u32[]{:S(2)}) copy-start(bf16[256,128]{1,0:T(8,128)(2,1)} %param.40) | copy-start | bytes 196612
  176.6 168.8 %reduce-scatter.27.cloned.1.call-start = ((), (), s32[]{:S(2)}) async-start(), calls=%async_computation.20 | async-start | bytes 3604480 | tf_op jit(solution)/shard_map/reduce_scatter | solution.py:49
  289.3 62.2 %copy-start.46 = (bf16[16,8]{0,1:T(8,128)(2,1)S(1)}, bf16[16,8]{0,1:T(8,128)(2,1)}, u32[]{:S(2)}) copy-start(bf16[16,8]{0,1:T(8,128)(2,1)} %param.43) | copy-start | bytes 772
  289.4 118.1 %all-gather.25.cloned.1.call-start = ((), (), s32[]{:S(2)}) async-start(), calls=%async_computation.21 | async-start | bytes 3604480 | tf_op jit(solution)/shard_map/all_gather | solution.py:43
  347.8 87.7 %all-gather.27.cloned.1.call-start = ((), (), s32[]{:S(2)}) async-start(), calls=%async_computation.22 | async-start | bytes 2359296 | tf_op jit(solution)/shard_map/all_gather | solution.py:172
  348.6 117.0 %all-gather.29.cloned.1.call-start = ((), (), s32[]{:S(2)}) async-start(), calls=%async_computation.23 | async-start | bytes 2359296 | tf_op jit(solution)/shard_map/all_gather | solution.py:173
  349.3 177.0 %all-gather.31.cloned.1.call-start = ((), (), s32[]{:S(2)}) async-start(), calls=%async_computation.25 | async-start | bytes 3604480 | tf_op jit(solution)/shard_map/all_gather | solution.py:55
  351.5 250.4 %reduce-scatter.31.cloned.1.call-start = ((), (), s32[]{:S(2)}) async-start(), calls=%async_computation.26 | async-start | bytes 3604480 | tf_op jit(solution)/shard_map/reduce_scatter | solution.py:60
  360.6 187.3 %copy-start.42 = (f32[1024]{0:T(1024)}, f32[1024]{0:T(1024)S(1)}, u32[]{:S(2)}) copy-start(f32[1024]{0:T(1024)S(1)} %reshape.345) | copy-start | bytes 12292
  376.0 67.8 %copy-start.35 = (f32[8,1024]{1,0:T(8,128)}, f32[8,1024]{1,0:T(8,128)S(1)}, u32[]{:S(2)}) copy-start(f32[8,1024]{1,0:T(8,128)S(1)} %fusion.118) | copy-start | bytes 98308
  547.4 112.9 %reduce-scatter.29.cloned.1.call-start = ((), (), s32[]{:S(2)}) async-start(), calls=%async_computation.24 | async-start | bytes 3604480 | tf_op jit(solution)/shard_map/reduce_scatter | solution.py:49
  556.7 167.3 %all-gather.33.cloned.1.call-start = ((), (), s32[]{:S(2)}) async-start(), calls=%async_computation.27 | async-start | bytes 3604480 | tf_op jit(solution)/shard_map/all_gather | solution.py:55
  665.0 149.6 %reduce-scatter.41.cloned.1.call-start = ((), (), s32[]{:S(2)}) async-start(), calls=%async_computation.32 | async-start | bytes 40960 | tf_op jit(solution)/shard_map/reduce_scatter | solution.py:63
  665.7 177.5 %reduce-scatter.33.cloned.1.call-start = ((), (), s32[]{:S(2)}) async-start(), calls=%async_computation.28 | async-start | bytes 3481600 | tf_op jit(solution)/shard_map/reduce_scatter | solution.py:294
  809.2 72.2 %reduce-scatter.35.cloned.1.call-start = ((), (), s32[]{:S(2)}) async-start(), calls=%async_computation.29 | async-start | bytes 3481600 | tf_op jit(solution)/shard_map/reduce_scatter | solution.py:300
  814.3 96.9 %reduce-scatter.39.cloned.1.call-start = ((), (), s32[]{:S(2)}) async-start(), calls=%async_computation.31 | async-start | bytes 40960 | tf_op jit(solution)/shard_map/reduce_scatter | solution.py:63
  819.7 28.7 %copy-start.7 = (f32[8,170,256]{1,2,0:T(8,128)S(1)}, f32[8,170,256]{1,2,0:T(8,128)}, u32[]{:S(2)}) copy-start(f32[8,170,256]{1,2,0:T(8,128)} %copy.210) | copy-start | bytes 4177924
  862.2 21.4 %copy-start.3 = (bf16[8,170,1024]{2,1,0:T(8,128)(2,1)S(1)}, bf16[8,170,1024]{2,1,0:T(8,128)(2,1)}, u32[]{:S(2)}) copy-start(bf16[8,170,1024]{2,1,0:T(8,128)(2,1)} %all-gather.19.cloned.1.call-done) | copy-start | bytes 8355844
  862.2 21.4 %copy-start.18 = (bf16[1024,256]{1,0:T(8,128)(2,1)S(1)}, bf16[1024,256]{1,0:T(8,128)(2,1)}, u32[]{:S(2)}) copy-start(bf16[1024,256]{1,0:T(8,128)(2,1)} %copy-done.17) | copy-start | bytes 1572868
  888.6 23.3 %copy-start.28 = (bf16[1024,16]{0,1:T(8,128)(2,1)S(1)}, bf16[1024,16]{0,1:T(8,128)(2,1)}, u32[]{:S(2)}) copy-start(bf16[1024,16]{0,1:T(8,128)(2,1)} %copy-done.27) | copy-start | bytes 98308
  892.1 158.0 %reduce-scatter.57.cloned.1.call-start = ((), (), s32[]{:S(2)}) async-start(), calls=%async_computation.40 | async-start | bytes 540672
  917.4 187.3 %reduce-scatter.37.cloned.1.call-start = ((), (), s32[]{:S(2)}) async-start(), calls=%async_computation.30 | async-start | bytes 3604480 | tf_op jit(solution)/shard_map/reduce_scatter | solution.py:60
  922.5 237.8 %reduce-scatter.53.cloned.1.call-start = ((), (), s32[]{:S(2)}) async-start(), calls=%async_computation.38 | async-start | bytes 4718592 | tf_op jit(solution)/shard_map/reduce_scatter | solution.py:363
  931.2 284.2 %reduce-scatter.55.cloned.1.call-start = ((), (), s32[]{:S(2)}) async-start(), calls=%async_computation.39 | async-start | bytes 4718592 | tf_op jit(solution)/shard_map/reduce_scatter | solution.py:364
  941.7 313.8 %reduce-scatter.45.cloned.1.call-start = ((), (), s32[]{:S(2)}) async-start(), calls=%async_computation.34 | async-start | bytes 1179648 | tf_op jit(solution)/shard_map/reduce_scatter | solution.py:359
  946.5 349.1 %reduce-scatter.51.cloned.1.call-start = ((), (), s32[]{:S(2)}) async-start(), calls=%async_computation.37 | async-start | bytes 1179648 | tf_op jit(solution)/shard_map/reduce_scatter | solution.py:362
  950.8 385.0 %reduce-scatter.47.cloned.1.call-start = ((), (), s32[]{:S(2)}) async-start(), calls=%async_computation.35 | async-start | bytes 1179648 | tf_op jit(solution)/shard_map/reduce_scatter | solution.py:360
  954.6 421.2 %reduce-scatter.49.cloned.1.call-start = ((), (), s32[]{:S(2)}) async-start(), calls=%async_computation.36 | async-start | bytes 1179648 | tf_op jit(solution)/shard_map/reduce_scatter | solution.py:361
  958.8 483.0 %reduce-scatter.43.cloned.1.call-start = ((), (), s32[]{:S(2)}) async-start(), calls=%async_computation.33 | async-start | bytes 7077888 | tf_op jit(solution)/shard_map/reduce_scatter | solution.py:358
  963.6 15.8 %copy-start.44 = (f32[256]{0:T(256)S(1)}, f32[256]{0:T(256)}, u32[]{:S(2)}) copy-start(f32[256]{0:T(256)} %get-tuple-element.331) | copy-start | bytes 3076
  963.6 18.0 %copy-start.11 = (bf16[8,170,4,64]{1,3,2,0:T(8,128)(2,1)S(1)}, bf16[8,170,4,64]{1,3,2,0:T(8,128)(2,1)}, u32[]{:S(2)}) copy-start(bf16[8,170,4,64]{1,3,2,0:T(8,128)(2,1)} %fusion.77) | copy-start | bytes 2088964
  963.6 18.3 %copy-start.14 = (bf16[8,170,256]{2,0,1:T(8,128)(2,1)S(1)}, bf16[8,170,256]{2,0,1:T(8,128)(2,1)}, u32[]{:S(2)}) copy-start(bf16[8,170,256]{2,0,1:T(8,128)(2,1)} %reduce-scatter.35.cloned.1.call-done) | copy-start | bytes 2088964
  963.7 86.5 %copy-start.52 = (s32[16]{0:T(128)S(1)}, s32[16]{0:T(128)}, u32[]{:S(2)}) copy-start(s32[16]{0:T(128)} %param.27) | copy-start | bytes 196
  963.7 141.1 %copy-start.13 = (bf16[8,170,256]{2,0,1:T(8,128)(2,1)S(1)}, bf16[8,170,256]{2,0,1:T(8,128)(2,1)}, u32[]{:S(2)}) copy-start(bf16[8,170,256]{2,0,1:T(8,128)(2,1)} %param.26) | copy-start | bytes 2088964
  963.7 141.1 %copy-start.16 = (bf16[8,170,256]{2,1,0:T(8,128)(2,1)S(1)}, bf16[8,170,256]{2,1,0:T(8,128)(2,1)}, u32[]{:S(2)}) copy-start(bf16[8,170,256]{2,1,0:T(8,128)(2,1)} %reduce-scatter.31.cloned.1.call-done) | copy-start | bytes 2088964
  1050.2 391.7 %copy-start.1 = (bf16[1001,32]{0,1:T(8,128)(2,1)S(1)}, bf16[1001,32]{0,1:T(8,128)(2,1)}, u32[]{:S(2)}) copy-start(bf16[1001,32]{0,1:T(8,128)(2,1)} %param.30) | copy-start | bytes 192196
  (34 other events, 219.7 us)
Sparse Core Ops, SparseCore 0:
  10.2 63.3 all-gather.18
  75.5 30.7 all-gather.16
  153.6 27.5 all-gather.22
  183.1 28.6 all-gather.20
  289.5 55.8 reduce-scatter.26
  348.0 59.5 all-gather.24
  409.4 26.0 all-gather.26
  437.4 28.1 all-gather.28
  467.2 59.1 all-gather.30
  547.6 54.3 reduce-scatter.30
  604.3 56.0 reduce-scatter.28
  665.1 58.9 all-gather.32
  726.9 17.0 reduce-scatter.40
  809.3 33.8 reduce-scatter.32
  845.7 35.6 reduce-scatter.34
  892.3 18.9 reduce-scatter.38
  917.5 132.5 reduce-scatter.56
  1052.4 52.2 reduce-scatter.36
  1109.1 51.1 reduce-scatter.52
  1164.0 51.2 reduce-scatter.54
  1219.4 36.0 reduce-scatter.44
  1259.6 36.0 reduce-scatter.50
  1299.7 36.0 reduce-scatter.46
  1339.7 36.0 reduce-scatter.48
  1380.1 61.7 reduce-scatter.42
where the time goes:
time: 1460 us; the launch traced here: 1450 us
  waiting for transfers between devices  831 us (57%)
  blocking collectives  256 us (18%)
  matrix products  208 us (14%)
  local copies, waits for them, and re-layouts  68.1 us (5%)
  other arithmetic  67.1 us (5%)
  between operations  15.9 us (1%)
    all_gather x2, waiting for transfers between devices, whole_grad(): return lax.all_gather(values, 'tp', axis=2, tiled=True)  119 us
    reduce_scatter x2, waiting for transfers between devices, branch_sum(): lax.psum_scatter(partial_rows.astype(jnp.bfloat16), 'tp', scatter_dimensi...  106 us
    dot_general x19, matrix products, product(): return jnp.einsum(form, left, right, preferred_element_type=jnp.float32)  93.3 us
    reduce_scatter x2, waiting for transfers between devices, row_grads(): lax.psum_scatter(partial_rows.astype(jnp.bfloat16), 'tp', scatter_dimensi...  89 us
    all_gather x1, blocking collectives, on_device(): lax.all_gather(cond_part, ('fsdp', 'ctx', 'tp'), axis=1, tiled=True)  76 us
    reduce_scatter x1, waiting for transfers between devices, on_device(): lax.psum_scatter(modulate_weight_part, ('fsdp', 'ctx'), scatter_dimension...  66.1 us
    reduce_scatter x1, waiting for transfers between devices, on_device(): lax.psum_scatter(down_weight_part, ('fsdp', 'ctx'), scatter_dimension=1,...  55.1 us
    reduce_scatter x1, waiting for transfers between devices, on_device(): lax.psum_scatter(up_weight_part, ('fsdp', 'ctx'), scatter_dimension=0, ti...  52.3 us
  transfers between devices with their start and end apart: 25, of which 20 were waited for; matrix products, arithmetic and copies ran while one was open for 15% of the time, Pallas kernels for 0%

commit v1 on v0

v1 whole, which is shorter than its diff:
```python
import functools
import math

import jax
import jax.numpy as jnp
from jax import lax
from jax.experimental import pallas as pl
from jax.experimental.pallas import tpu as pltpu
from jax.sharding import PartitionSpec as P

HD = 64
GC = 512
MESH = pl.DeviceIdType.MESH
precise = lax.Precision.HIGHEST
norm_epsilon = 1e-06
clip_threshold = 2.0
masked_score = -1e30
f32, bf16 = jnp.float32, jnp.bfloat16


def product(left, right, form):
    return jnp.einsum(form, left, right, preferred_element_type=f32)


def rcopy(src, dst, send_sem, recv_sem, device):
    return pltpu.make_async_remote_copy(
        src_ref=src,
        dst_ref=dst,
        send_sem=send_sem,
        recv_sem=recv_sem,
        device_id=device,
        device_id_type=MESH,
    )


class Place:
    def __init__(self, fs, cs, ts):
        self.fs, self.cs, self.ts = fs, cs, ts
        self.count = fs * cs * ts
        self.f, self.c, self.t = (lax.axis_index(n) for n in ("fsdp", "ctx", "tp"))
        self.hi, self.k = self.c // 2, lax.rem(self.c, 2)
        self.me = (self.f * cs + self.c) * ts + self.t
        self.slot = self.hi * ts + self.t

    def coords(self, n):
        return (n // (self.cs * self.ts), lax.rem(n // self.ts, self.cs), lax.rem(n, self.ts))

    def sibling(self):
        return (self.f, self.hi * 2 + 1 - self.k, self.t)

    def ypeer(self):
        return (self.f, (1 - self.hi) * 2 + self.k, self.t)

    def xpeer(self, s):
        return (lax.rem(self.f + s, self.fs), self.c, self.t)

    def xfrom(self, s):
        return lax.rem(self.f + self.fs - s, self.fs)

    def zpeer(self, s):
        return (self.f, self.c, lax.rem(self.t + s, self.ts))

    def zto(self, s):
        return lax.rem(self.t + s, self.ts)

    def zfrom(self, s):
        return lax.rem(self.t + self.ts - s, self.ts)

    def barrier(self):
        sem = pltpu.get_barrier_semaphore()

        def greet(n, carry):
            @pl.when(n != self.me)
            def _():
                pl.semaphore_signal(sem, inc=1, device_id=self.coords(n), device_id_type=MESH)

            return carry

        lax.fori_loop(0, self.count, greet, 0)
        pl.semaphore_wait(sem, self.count - 1)


def exchange_images(at, src_of, dst_of, send_sems, recv_sems, local_sem):
    slots = 2 * at.ts

    def start():
        for i in range(slots):
            hi, t = i // at.ts, i % at.ts

            @pl.when(i != at.slot)
            def _():
                rcopy(
                    src_of(i),
                    dst_of(at.slot),
                    send_sems.at[i],
                    recv_sems.at[at.slot],
                    (at.f, hi * 2 + at.k, t),
                ).start()

            @pl.when(i == at.slot)
            def _():
                pltpu.make_async_copy(src_of(i), dst_of(i), local_sem).start()

    def wait():
        for i in range(slots):
            @pl.when(i != at.slot)
            def _():
                rcopy(src_of(i), dst_of(i), send_sems.at[i], recv_sems.at[i], (at.f, at.c, at.t)).wait()

            @pl.when(i == at.slot)
            def _():
                pltpu.make_async_copy(src_of(i), dst_of(i), local_sem).wait()

    return start, wait


def broadcast_messages(at, src_of, slot_of, send_sems, recv_sems, local_sem):
    def start():
        def each(n, carry):
            @pl.when(n != at.me)
            def _():
                rcopy(src_of(n), slot_of(at.me), send_sems.at[n], recv_sems.at[at.me], at.coords(n)).start()

            @pl.when(n == at.me)
            def _():
                pltpu.make_async_copy(src_of(n), slot_of(n), local_sem).start()

            return carry

        lax.fori_loop(0, at.count, each, 0)

    def wait():
        def each(n, carry):
            @pl.when(n != at.me)
            def _():
                rcopy(src_of(n), slot_of(n), send_sems.at[n], recv_sems.at[n], at.coords(n)).wait()

            @pl.when(n == at.me)
            def _():
                pltpu.make_async_copy(src_of(n), slot_of(n), local_sem).wait()

            return carry

        lax.fori_loop(0, at.count, each, 0)

    return start, wait


def gather_kernel(
    fs, cs, ts, padded, per,
    x_ref, g_ref, s1, s2, s3, cond_ref, wm_ref, small_ref,
    xo, go, w1, w2, w3, mo,
    cond_slots, part,
    x_send, x_recv, g_send, g_recv, loc, sib_send, sib_recv, gsib_send, gsib_recv,
    c_send, c_recv, m_send, m_recv,
    core_send, core_recv, core_loc, z_send, z_recv, xs_send, xs_recv, ys_send, ys_recv,
    fx_send, fx_recv, fy_send, fy_recv,
):
    at = Place(fs, cs, ts)
    at.barrier()
    width = x_ref.shape[2]
    shards, weights = (s1, s2, s3), (w1, w2, w3)
    half = ts // 2

    def block_at(out):
        def dst(i):
            c = (i // ts) * 2 + at.k
            return out.at[pl.ds(c * padded, padded), pl.ds(pl.multiple_of(lax.rem(i, ts) * width, 128), width)]

        return dst

    x_start, x_wait = exchange_images(at, lambda i: x_ref.at[i], block_at(xo), x_send, x_recv, loc.at[0])
    g_start, g_wait = exchange_images(at, lambda i: g_ref.at[i], block_at(go), g_send, g_recv, loc.at[1])
    x_start()

    def row(f, hi, k=0):
        return pl.multiple_of(((f * 2 + hi) * 2 + k) * per, per)

    def core_copies(g):
        mine = weights[g].at[at.t, pl.ds(row(at.f, at.hi, at.k), per), :]
        theirs = weights[g].at[at.t, pl.ds(row(at.f, at.hi, 1 - at.k), per), :]
        local = pltpu.make_async_copy(shards[g].at[at.k], mine, core_loc.at[g])
        out = rcopy(shards[g].at[1 - at.k], mine, core_send.at[g], core_recv.at[g], at.sibling())
        inn = rcopy(shards[g].at[1 - at.k], theirs, core_send.at[g], core_recv.at[g], at.sibling())
        return local, out, inn

    def core_start(g):
        local, out, _ = core_copies(g)
        local.start()
        out.start()

    def core_wait(g):
        local, _, inn = core_copies(g)
        local.wait()
        inn.wait()

    def slab(g, z, n, f, hi):
        return weights[g].at[pl.ds(z, n), pl.ds(row(f, hi), 2 * per), :]

    def z_start(g):
        for s in range(1, ts):
            src = slab(g, at.t, 1, at.f, at.hi)
            rcopy(src, src, z_send.at[g, s], z_recv.at[g, s], at.zpeer(s)).start()

    def z_wait(g):
        for s in range(1, ts):
            src = slab(g, at.zfrom(s), 1, at.f, at.hi)
            rcopy(src, src, z_send.at[g, s], z_recv.at[g, s], at.zpeer(s)).wait()

    def xy_start(g):
        src = slab(g, 0, ts, at.f, at.hi)
        rcopy(src, src, ys_send.at[g], ys_recv.at[g], at.ypeer()).start()
        for s in range(1, fs):
            rcopy(src, src, xs_send.at[g, s], xs_recv.at[g, s], at.xpeer(s)).start()

    def xy_wait(g):
        src = slab(g, 0, ts, at.f, 1 - at.hi)
        rcopy(src, src, ys_send.at[g], ys_recv.at[g], at.ypeer()).wait()
        for s in range(1, fs):
            src = slab(g, 0, ts, at.xfrom(s), at.hi)
            rcopy(src, src, xs_send.at[g, s], xs_recv.at[g, s], at.xpeer(s)).wait()

    def fwd_start(g):
        for s in range(1, fs):
            src = slab(g, half, half, at.f, 1 - at.hi)
            rcopy(src, src, fx_send.at[g, s], fx_recv.at[g, s], at.xpeer(s)).start()
            src = slab(g, 0, half, at.xfrom(s), at.hi)
            rcopy(src, src, fy_send.at[g, s], fy_recv.at[g, s], at.ypeer()).start()

    def fwd_wait(g):
        for s in range(1, fs):
            src = slab(g, half, half, at.xfrom(s), 1 - at.hi)
            rcopy(src, src, fx_send.at[g, s], fx_recv.at[g, s], at.xpeer(s)).wait()
            src = slab(g, 0, half, at.xfrom(s), 1 - at.hi)
            rcopy(src, src, fy_send.at[g, s], fy_recv.at[g, s], at.ypeer()).wait()

    core_start(0)

    cond_slots[at.t] = cond_ref[...]

    def cond_copy(s, slot):
        return rcopy(cond_ref, cond_slots.at[slot], c_send.at[s], c_recv.at[s], at.zpeer(s))

    for s in range(1, ts):
        cond_copy(s, at.t).start()
    core_start(1)
    core_start(2)
    for s in range(1, ts):
        cond_copy(s, at.zfrom(s)).wait()
    cond = cond_slots[0]
    for z in range(1, ts):
        cond = cond + cond_slots[z]
    silu = (cond / (1.0 + jnp.exp(-cond))).astype(bf16)
    columns = width
    for j in range(6):
        part[:, j, :] = jnp.dot(silu, wm_ref[:, j * columns : (j + 1) * columns], preferred_element_type=f32)
    images = part.shape[0]
    for j in range(2):
        part[:, 6 + j, :] = jnp.broadcast_to(small_ref[j : j + 1, :], (images, columns))

    def image_of(n):
        f, c, t = at.coords(n)
        return (f * 2 + c // 2) * ts + t

    m_start, m_wait = broadcast_messages(
        at, lambda n: part.at[image_of(n)], lambda n: mo.at[n], m_send, m_recv, loc.at[2]
    )
    m_start()

    core_wait(0)
    z_start(0)
    x_wait()

    def sib_copies(out, send, recv):
        copies = []
        for hi in range(2):
            mine = out.at[pl.ds((hi * 2 + at.k) * padded, padded), :]
            theirs = out.at[pl.ds((hi * 2 + 1 - at.k) * padded, padded), :]
            copies.append(
                (
                    rcopy(mine, mine, send.at[hi], recv.at[hi], at.sibling()),
                    rcopy(theirs, theirs, send.at[hi], recv.at[hi], at.sibling()),
                )
            )
        return copies

    for out, _ in sib_copies(xo, sib_send, sib_recv):
        out.start()
    g_start()
    core_wait(1)
    core_wait(2)
    z_wait(0)
    xy_start(0)
    z_start(1)
    z_wait(1)
    xy_start(1)
    xy_wait(0)
    fwd_start(0)
    z_start(2)
    z_wait(2)
    xy_wait(1)
    xy_start(2)
    fwd_start(1)
    g_wait()
    for out, _ in sib_copies(go, gsib_send, gsib_recv):
        out.start()
    xy_wait(2)
    fwd_start(2)
    m_wait()
    for _, inn in sib_copies(xo, sib_send, sib_recv):
        inn.wait()
    for _, inn in sib_copies(go, gsib_send, gsib_recv):
        inn.wait()
    for g in range(3):
        fwd_wait(g)


def scatter_kernel(
    fs, cs, ts, padded, per,
    d1, d2, d3, dx_ref, bo_ref, small_ref,
    o1, o2, o3, dxo, boo, mo,
    ry1, rx1, xs, ys, rx2, ry2, own, rz, total,
    dx_send, dx_recv, bo_send, bo_recv, loc, m_send, m_recv,
    y1_send, y1_recv, x1_send, x1_recv, x2_send, x2_recv, y2_send, y2_recv,
    z_send, z_recv, k_send, k_recv,
):
    at = Place(fs, cs, ts)
    at.barrier()
    width = dxo.shape[2]
    grads, outs = (d1, d2, d3), (o1, o2, o3)
    half = ts // 2

    def block_of(ref):
        def src(i):
            c = (i // ts) * 2 + at.k
            return ref.at[pl.ds(c * padded, padded), pl.ds(pl.multiple_of(lax.rem(i, ts) * width, 128), width)]

        return src

    dx_start, dx_wait = exchange_images(at, block_of(dx_ref), lambda i: dxo.at[i], dx_send, dx_recv, loc.at[0])
    bo_start, bo_wait = exchange_images(at, block_of(bo_ref), lambda i: boo.at[i], bo_send, bo_recv, loc.at[1])

    def message_slot(n):
        f, c, t = at.coords(n)
        return mo.at[(f * 2 + c // 2) * ts + t, lax.rem(c, 2)]

    m_start, m_wait = broadcast_messages(
        at, lambda n: small_ref.at[lax.rem(n, ts)], message_slot, m_send, m_recv, loc.at[2]
    )

    def row(f, hi):
        return pl.multiple_of((f * 2 + hi) * 2 * per, 2 * per)

    def slab(g, z, n, f, hi):
        return grads[g].at[pl.ds(z, n), pl.ds(row(f, hi), 2 * per), :]

    def far(s):
        return lax.rem(at.f + s, fs)

    def one(g, s):
        a = rcopy(slab(g, 0, half, far(s), 1 - at.hi), ry1.at[g, s - 1], y1_send.at[g, s], y1_recv.at[g, s], at.ypeer())
        b = rcopy(slab(g, half, half, far(s), 1 - at.hi), rx1.at[g, s - 1], x1_send.at[g, s], x1_recv.at[g, s], at.xpeer(s))
        return a, b

    def two_x(g, s):
        return rcopy(xs.at[g, s - 1], rx2.at[g, s - 1], x2_send.at[g, s], x2_recv.at[g, s], at.xpeer(s))

    def two_y(g):
        return rcopy(ys.at[g], ry2.at[g], y2_send.at[g], y2_recv.at[g], at.ypeer())

    def three(g, s):
        return rcopy(own.at[g, at.zto(s)], rz.at[g, s - 1], z_send.at[g, s], z_recv.at[g, s], at.zpeer(s))

    def start_one(g):
        for s in range(1, fs):
            for copy in one(g, s):
                copy.start()

    def start_two(g):
        for s in range(1, fs):
            for copy in one(g, s):
                copy.wait()

        def body(z, carry):
            for s in range(1, fs):
                value = grads[g][z, pl.ds(row(far(s), at.hi), 2 * per), :].astype(f32)
                value = value + ry1[g, s - 1, z].astype(f32)
                xs[g, s - 1, z] = value.astype(bf16)
                xs[g, s - 1, half + z] = grads[g][half + z, pl.ds(row(far(s), at.hi), 2 * per), :]
            value = grads[g][half + z, pl.ds(row(at.f, 1 - at.hi), 2 * per), :].astype(f32)
            for s in range(1, fs):
                value = value + rx1[g, s - 1, z].astype(f32)
            ys[g, half + z] = value.astype(bf16)
            ys[g, z] = grads[g][z, pl.ds(row(at.f, 1 - at.hi), 2 * per), :]
            return carry

        lax.fori_loop(0, half, body, 0)
        for s in range(1, fs):
            two_x(g, s).start()
        two_y(g).start()

    def start_three(g):
        for s in range(1, fs):
            two_x(g, s).wait()
        two_y(g).wait()

        def body(z, carry):
            value = grads[g][z, pl.ds(row(at.f, at.hi), 2 * per), :].astype(f32) + ry2[g, z].astype(f32)
            for s in range(1, fs):
                value = value + rx2[g, s - 1, z].astype(f32)
            own[g, z] = value.astype(bf16)
            return carry

        lax.fori_loop(0, ts, body, 0)
        for s in range(1, ts):
            three(g, s).start()

    def four(g):
        there = pl.multiple_of((1 - at.k) * per, per)
        out = rcopy(total.at[g, pl.ds(there, per)], outs[g].at[at.k], k_send.at[g], k_recv.at[g], at.sibling())
        inn = rcopy(total.at[g, pl.ds(there, per)], outs[g].at[1 - at.k], k_send.at[g], k_recv.at[g], at.sibling())
        return out, inn

    def start_four(g):
        for s in range(1, ts):
            three(g, s).wait()
        value = own[g, at.t].astype(f32)
        for s in range(1, ts):
            value = value + rz[g, s - 1].astype(f32)
        total[g] = value
        four(g)[0].start()
        outs[g][at.k] = total[g, pl.ds(pl.multiple_of(at.k * per, per), per), :]

    order = (2, 1, 0)
    start_one(order[0])
    m_start()
    start_one(order[1])
    start_two(order[0])
    start_one(order[2])
    start_two(order[1])
    start_three(order[0])
    start_two(order[2])
    bo_start()
    start_three(order[1])
    start_four(order[0])
    dx_start()
    start_three(order[2])
    start_four(order[1])
    start_four(order[2])
    for g in range(3):
        four(g)[1].wait()
    m_wait()
    bo_wait()
    dx_wait()


def attention_forward(q_ref, k_ref, v_ref, qg_ref, kg_ref, sq_ref, sk_ref, qh_ref, kh_ref, at_ref, lse_ref, hm_ref):
    rows = q_ref.shape[0]
    tile = rows // 4
    for h in range(2):
        lanes = slice(h * HD, (h + 1) * HD)
        q, k = q_ref[:, lanes], k_ref[:, lanes]
        qh = q * lax.rsqrt(jnp.mean(q * q, axis=-1, keepdims=True) + norm_epsilon) * qg_ref[0, :, lanes]
        kh = k * lax.rsqrt(jnp.mean(k * k, axis=-1, keepdims=True) + norm_epsilon) * kg_ref[0, :, lanes]
        qh_ref[:, lanes] = qh.astype(bf16)
        kh_ref[:, lanes] = kh.astype(bf16)
        highest = jnp.full((1, 1), -jnp.inf, f32)
        keys, vals = kh_ref[:, lanes], v_ref[:, lanes]
        for n in range(4):
            span = slice(n * tile, (n + 1) * tile)
            s = lax.dot_general(qh_ref[span, lanes], keys, (((1,), (1,)), ((), ())), preferred_element_type=f32) * 0.125
            allowed = sk_ref[...] <= sq_ref[span, :]
            highest = jnp.maximum(highest, jnp.max(jnp.where(allowed, s, -jnp.inf), keepdims=True))
            s = jnp.where(allowed, s, masked_score)
            peak = jnp.max(s, axis=-1, keepdims=True)
            e = jnp.exp(s - peak)
            total = jnp.sum(e, axis=-1, keepdims=True)
            log_total = peak + jnp.log(total)
            p = jnp.exp(s - log_total).astype(bf16)
            at_ref[span, lanes] = jnp.dot(p, vals, preferred_element_type=f32).astype(bf16)
            lse_ref[0, h, span, :] = log_total
        hm_ref[0, h] = jnp.broadcast_to(highest, (8, 128))


def attention_backward(
    q_ref, k_ref, qh_ref, kh_ref, v_ref, da_ref, lse_ref, qg_ref, kg_ref, sq_ref, sk_ref,
    dq_ref, dk_ref, dv_ref, gg_ref, dqh, dkh, dvh,
):
    rows = q_ref.shape[0]
    tile = rows // 4
    for h in range(2):
        lanes = slice(h * HD, (h + 1) * HD)
        keys, vals = kh_ref[:, lanes], v_ref[:, lanes]
        dkh[...] = jnp.zeros_like(dkh)
        dvh[...] = jnp.zeros_like(dvh)
        for n in range(4):
            span = slice(n * tile, (n + 1) * tile)
            qh, da = qh_ref[span, lanes], da_ref[span, lanes]
            s = lax.dot_general(qh, keys, (((1,), (1,)), ((), ())), preferred_element_type=f32) * 0.125
            allowed = sk_ref[...] <= sq_ref[span, :]
            p = jnp.where(allowed, jnp.exp(jnp.where(allowed, s, masked_score) - lse_ref[0, h, span, :]), 0.0)
            dp = lax.dot_general(da, vals, (((1,), (1,)), ((), ())), preferred_element_type=f32)
            centre = jnp.sum(p * dp, axis=-1, keepdims=True)
            ds = (p * (dp - centre)).astype(bf16)
            dqh[span, :] = jnp.dot(ds, keys, preferred_element_type=f32) * 0.125
            dkh[...] += lax.dot_general(ds, qh, (((0,), (0,)), ((), ())), preferred_element_type=f32)
            dvh[...] += lax.dot_general(p.astype(bf16), da, (((0,), (0,)), ((), ())), preferred_element_type=f32)
        dv_ref[:, lanes] = dvh[...].astype(bf16)
        for which, (raw_ref, gain_ref, delta, out_ref) in enumerate(
            ((q_ref, qg_ref, dqh[...], dq_ref), (k_ref, kg_ref, dkh[...] * 0.125, dk_ref))
        ):
            raw, gain = raw_ref[:, lanes], gain_ref[0, :, lanes]
            r = lax.rsqrt(jnp.mean(raw * raw, axis=-1, keepdims=True) + norm_epsilon)
            gg_ref[0, which : which + 1, lanes] = jnp.sum(delta * raw * r, axis=0, keepdims=True)
            t = delta * gain
            out_ref[:, lanes] = (r * t - raw * (r * r * r) * jnp.mean(t * raw, axis=-1, keepdims=True)).astype(bf16)


def layer_norm(values):
    centered = values - jnp.mean(values, axis=-1, keepdims=True)
    spread = jnp.mean(centered * centered, axis=-1, keepdims=True)
    return centered * lax.rsqrt(spread + norm_epsilon), lax.rsqrt(spread + norm_epsilon)


def norm_backward(normal, inverse, scale, incoming):
    e = incoming * (1.0 + scale)
    mean_e = jnp.mean(e, axis=-1, keepdims=True)
    mean_en = jnp.mean(e * normal, axis=-1, keepdims=True)
    return (
        (e - mean_e - normal * mean_en) * inverse,
        jnp.sum(incoming, axis=0),
        jnp.sum(incoming * normal, axis=0),
    )


def gelu_tanh(values):
    return jax.nn.gelu(values, approximate=True)


def on_device(
    fs, cs, ts,
    inputs, cotangent, labels, scale_ids, head_flags, class_table, modulate_weight, modulate_bias,
    query_weight, key_weight, value_weight, query_bias, value_bias, query_gain, key_gain,
    output_weight, output_bias, up_weight, up_bias, down_weight, down_bias,
):
    images, rows_here, width = inputs.shape
    if images != 2 * ts or cs != 4 or ts % 2 or width != 256:
        raise ValueError("unsupported mesh")
    length = scale_ids.shape[0]
    every = labels.shape[0]
    count = fs * cs * ts
    blocks = fs * cs
    padded = -(-rows_here // 16) * 16
    tokens = cs * padded
    features = ts * width
    per = query_weight.shape[0]
    part_cols = class_table.shape[1]
    f, c, t = (lax.axis_index(n) for n in ("fsdp", "ctx", "tp"))
    core = lax.rem(c, 2)

    classes = class_table.shape[0]
    onehot = (labels[:, None] == jnp.arange(classes, dtype=jnp.int32)[None, :]).astype(bf16)
    cond_part = jnp.dot(onehot, class_table, preferred_element_type=f32)
    cond_spread = lax.dynamic_update_slice(
        jnp.zeros((every, per), f32), cond_part, (0, t * part_cols)
    )
    fit = ((0, 0), (0, padded - rows_here), (0, 0))
    x_blocks, g_blocks = jnp.pad(inputs, fit), jnp.pad(cotangent, fit)

    def halves(weight):
        return weight.reshape(per, 2, -1).transpose(1, 0, 2)

    out_t, down_t = output_weight.T, down_weight.T
    shard_one = jnp.concatenate(
        [halves(query_weight), halves(key_weight), halves(value_weight), halves(out_t)], axis=2
    )
    shard_two, shard_three = halves(up_weight), halves(down_t)
    lanes = modulate_bias.shape[2]
    small_rows = jnp.concatenate(
        [
            modulate_bias.reshape(-1, lanes), query_bias, value_bias, query_gain, key_gain,
            output_bias, down_bias, up_bias,
        ],
        axis=0,
    ).astype(f32)
    small = jnp.pad(small_rows.reshape(-1), (0, 2 * width - small_rows.size)).reshape(2, width)
    any_spec = pl.BlockSpec(memory_space=pl.ANY)
    vmem_spec = pl.BlockSpec(memory_space=pltpu.VMEM)
    dma = pltpu.SemaphoreType.DMA
    slots = 2 * ts
    wide = jax.ShapeDtypeStruct((ts, features, GC), bf16)
    flat = jax.ShapeDtypeStruct((tokens, features), bf16)
    x, g, weight_one, weight_two, weight_three, messages = pl.pallas_call(
        functools.partial(gather_kernel, fs, cs, ts, padded, per),
        name="gather",
        out_shape=(flat, flat, wide, wide, wide, jax.ShapeDtypeStruct((count, 8, width), f32)),
        in_specs=[any_spec] * 5 + [vmem_spec] * 3,
        out_specs=(any_spec,) * 5 + (vmem_spec,),
        scratch_shapes=[
            pltpu.VMEM((ts, every, per), f32),
            pltpu.VMEM((every, 8, width), f32),
            dma((slots,)), dma((slots,)), dma((slots,)), dma((slots,)), dma((3,)),
            dma((2,)), dma((2,)), dma((2,)), dma((2,)),
            dma((ts,)), dma((ts,)), dma((count,)), dma((count,)),
            dma((3,)), dma((3,)), dma((3,)), dma((3, ts)), dma((3, ts)),
            dma((3, fs)), dma((3, fs)), dma((3,)), dma((3,)),
            dma((3, fs)), dma((3, fs)), dma((3, fs)), dma((3, fs)),
        ],
        compiler_params=pltpu.CompilerParams(
            collective_id=0, has_side_effects=True, vmem_limit_bytes=32 << 20
        ),
    )(
        x_blocks, g_blocks, shard_one, shard_two, shard_three, cond_spread,
        modulate_weight.reshape(per, 6 * width), small,
    )

    messages = messages.reshape(blocks, ts, 8, width)
    params = messages[:, :, 6:8].reshape(blocks, ts, 2 * width)[:, :, : small_rows.size]
    params = params.reshape(blocks, ts, -1, lanes).transpose(2, 1, 0, 3)
    params = params.reshape(-1, ts, blocks * lanes)
    heads = modulate_bias.shape[1]

    def whole(start):
        return params[start : start + heads].transpose(1, 0, 2).reshape(features)

    def here(start, rows):
        mine = lax.dynamic_slice_in_dim(params, start + core * (rows // 2), rows // 2, 0)
        return mine.transpose(1, 0, 2).reshape(ts, 1, -1)

    first = 6 * heads
    query_shift, value_shift = here(first, heads), here(first + heads, heads)
    query_gains, key_gains = here(first + 2 * heads, heads), here(first + 3 * heads, heads)
    output_shift, down_shift = whole(first + 4 * heads), whole(first + 5 * heads)
    up_shift = here(first + 6 * heads, up_bias.shape[0])
    modulate_shift = (
        params[:first].reshape(6, heads, ts, -1).transpose(0, 2, 1, 3).reshape(6, features)
    )
    modulation = jnp.sum(messages[:, :, :6], axis=0).transpose(1, 0, 2).reshape(6, features)
    modulation = (modulation + modulate_shift).astype(bf16).astype(f32)
    shift_one, scale_one, gate_one, shift_two, scale_two, gate_two = (modulation[j] for j in range(6))

    x_wide = x.astype(f32)
    valid = (jnp.arange(tokens) % padded < rows_here)[:, None]
    x_wide = jnp.where(valid, x_wide, 0.0)
    incoming = jnp.where(valid, g.astype(f32), 0.0)
    normal_one, inverse_one = layer_norm(x_wide)
    normed_one = (normal_one * (1.0 + scale_one) + shift_one).astype(bf16)
    qkv_pre = product(normed_one, weight_one[:, :, :384], "sd,zde->sze")
    query_pre = (qkv_pre[:, :, :128] + query_shift[:, 0]).reshape(tokens, -1)
    key_pre = qkv_pre[:, :, 128:256].reshape(tokens, -1)
    value_rows = (qkv_pre[:, :, 256:] + value_shift[:, 0]).astype(bf16).reshape(tokens, -1)
    ids = scale_ids.reshape(cs, rows_here)
    spare = ((0, 0), (0, padded - rows_here))
    ids_query = jnp.pad(ids, spare, constant_values=-1).reshape(tokens, 1)
    ids_key = jnp.pad(ids, spare, constant_values=1 << 20).reshape(1, tokens)
    column = pl.BlockSpec((tokens, 128), lambda z: (0, z))
    gain_spec = pl.BlockSpec((1, 1, 128), lambda z: (z, 0, 0))
    id_specs = [pl.BlockSpec((tokens, 1), lambda z: (0, 0)), pl.BlockSpec((1, tokens), lambda z: (0, 0))]
    lse_spec = pl.BlockSpec((1, 2, tokens, 1), lambda z: (z, 0, 0, 0))
    here_cols = ts * 128
    rows_type = jax.ShapeDtypeStruct((tokens, here_cols), bf16)
    query_hat, key_hat, attended, log_totals, highest = pl.pallas_call(
        attention_forward,
        name="attend",
        grid=(ts,),
        out_shape=(
            rows_type, rows_type, rows_type,
            jax.ShapeDtypeStruct((ts, 2, tokens, 1), f32),
            jax.ShapeDtypeStruct((ts, 2, 8, 128), f32),
        ),
        in_specs=[column] * 3 + [gain_spec] * 2 + id_specs,
        out_specs=(column, column, column, lse_spec, pl.BlockSpec((1, 2, 8, 128), lambda z: (z, 0, 0, 0))),
        compiler_params=pltpu.CompilerParams(vmem_limit_bytes=48 << 20),
    )(query_pre, key_pre, value_rows, query_gains, key_gains, ids_query, ids_key)

    pairs = [(i, i ^ 1) for i in range(cs)]

    def both_cores(partial_rows):
        mine = partial_rows.astype(bf16)
        return mine.astype(f32) + lax.ppermute(mine, "ctx", pairs).astype(f32)

    attended_z = attended.reshape(tokens, ts, 128)
    branch_one = both_cores(product(attended_z, weight_one[:, :, 384:], "sze,zfe->sf")) + output_shift
    middle = (x_wide + gate_one * branch_one).astype(bf16)
    middle_wide = middle.astype(f32)
    normal_two, inverse_two = layer_norm(middle_wide)
    normed_two = (normal_two * (1.0 + scale_two) + shift_two).astype(bf16)
    hidden_pre = product(normed_two, weight_two, "sd,zdh->zsh") + up_shift
    hidden = gelu_tanh(hidden_pre).astype(bf16)
    branch_two = both_cores(product(hidden, weight_three, "zsh,zfh->sf")) + down_shift
    block_rows = (middle_wide + gate_two * branch_two).astype(bf16)

    down_delta = (incoming * gate_two).astype(bf16)
    gate_two_delta = jnp.sum(incoming * branch_two, axis=0)
    down_bias_part = jnp.sum(down_delta.astype(f32), axis=0)
    grad_three = product(down_delta, hidden, "sf,zsh->zfh").astype(bf16)
    hidden_delta = product(down_delta, weight_three, "sf,zfh->zsh")
    primal, gelu_back = jax.vjp(gelu_tanh, hidden_pre)
    pre_delta = gelu_back(hidden_delta)[0].astype(bf16)
    up_bias_part = jnp.sum(pre_delta.astype(f32), axis=1)
    grad_two = product(normed_two, pre_delta, "sd,zsh->zdh").astype(bf16)
    normed_two_delta = both_cores(product(pre_delta, weight_two, "zsh,zdh->sd"))
    middle_part, shift_two_delta, scale_two_delta = norm_backward(
        normal_two, inverse_two, scale_two, normed_two_delta
    )
    middle_delta = incoming + middle_part
    branch_delta = (middle_delta * gate_one).astype(bf16)
    gate_one_delta = jnp.sum(middle_delta * branch_one, axis=0)
    output_bias_part = jnp.sum(branch_delta.astype(f32), axis=0)
    grad_out = product(branch_delta, attended_z, "sf,sze->zfe").astype(bf16)
    attended_delta = product(branch_delta, weight_one[:, :, 384:], "sf,zfe->sze").astype(bf16)
    queries_delta, keys_delta, values_low, gain_parts = pl.pallas_call(
        attention_backward,
        name="attend_back",
        grid=(ts,),
        out_shape=(rows_type, rows_type, rows_type, jax.ShapeDtypeStruct((ts, 2, 128), f32)),
        in_specs=[column] * 6 + [lse_spec] + [gain_spec] * 2 + id_specs,
        out_specs=(column, column, column, pl.BlockSpec((1, 2, 128), lambda z: (z, 0, 0))),
        scratch_shapes=[pltpu.VMEM((tokens, HD), f32)] * 3,
        compiler_params=pltpu.CompilerParams(vmem_limit_bytes=48 << 20),
    )(
        query_pre, key_pre, query_hat, key_hat, value_rows,
        attended_delta.reshape(tokens, here_cols), log_totals, query_gains, key_gains, ids_query, ids_key,
    )
    query_bias_part = jnp.sum(queries_delta.astype(f32), axis=0).reshape(ts, 128)
    value_bias_part = jnp.sum(values_low.astype(f32), axis=0).reshape(ts, 128)
    deltas = jnp.concatenate(
        [v.reshape(tokens, ts, 128) for v in (queries_delta, keys_delta, values_low)], axis=2
    )
    grad_qkv = product(normed_one, deltas, "sd,sze->zde").astype(bf16)
    grad_one = jnp.concatenate([grad_qkv, grad_out], axis=2)
    normed_one_delta = both_cores(product(deltas, weight_one[:, :, :384], "sze,zde->sd"))
    inputs_part, shift_one_delta, scale_one_delta = norm_backward(
        normal_one, inverse_one, scale_one, normed_one_delta
    )
    inputs_delta = (middle_delta + inputs_part).astype(bf16)
    deltas_six = jnp.stack(
        [shift_one_delta, scale_one_delta, gate_one_delta, shift_two_delta, scale_two_delta, gate_two_delta]
        + [output_bias_part, down_bias_part]
    )
    tops = jnp.broadcast_to(highest[:, :, 0, :1], (ts, 2, HD)).reshape(ts, 1, 128)
    own_small = jnp.concatenate(
        [
            deltas_six.reshape(8, ts, width).transpose(1, 0, 2),
            jnp.stack([query_bias_part, value_bias_part], axis=1).reshape(ts, 1, width),
            gain_parts.reshape(ts, 1, width),
            up_bias_part.reshape(ts, 2, width),
            jnp.pad(tops, ((0, 0), (0, 3), (0, width - 128))),
        ],
        axis=1,
    )
    f1 = max(fs - 1, 1)
    out_type = jax.ShapeDtypeStruct((2, per, GC), f32)
    blocks_type = jax.ShapeDtypeStruct((slots, padded, width), bf16)
    sum_one, sum_two, sum_three, dx_blocks, bo_blocks, mail = pl.pallas_call(
        functools.partial(scatter_kernel, fs, cs, ts, padded, per),
        name="scatter",
        out_shape=(
            out_type, out_type, out_type, blocks_type, blocks_type,
            jax.ShapeDtypeStruct((every, 2, 16, width), f32),
        ),
        in_specs=[vmem_spec] * 3 + [any_spec] * 3,
        out_specs=(vmem_spec,) * 3 + (any_spec,) * 3,
        scratch_shapes=[
            pltpu.VMEM((3, f1, ts // 2, 2 * per, GC), bf16),
            pltpu.VMEM((3, f1, ts // 2, 2 * per, GC), bf16),
            pltpu.VMEM((3, f1, ts, 2 * per, GC), bf16),
            pltpu.VMEM((3, ts, 2 * per, GC), bf16),
            pltpu.VMEM((3, f1, ts, 2 * per, GC), bf16),
            pltpu.VMEM((3, ts, 2 * per, GC), bf16),
            pltpu.VMEM((3, ts, 2 * per, GC), bf16),
            pltpu.VMEM((3, ts - 1, 2 * per, GC), bf16),
            pltpu.VMEM((3, 2 * per, GC), f32),
            dma((slots,)), dma((slots,)), dma((slots,)), dma((slots,)), dma((3,)),
            dma((count,)), dma((count,)),
            dma((3, fs)), dma((3, fs)), dma((3, fs)), dma((3, fs)),
            dma((3, fs)), dma((3, fs)), dma((3,)), dma((3,)),
            dma((3, ts)), dma((3, ts)), dma((3,)), dma((3,)),
        ],
        compiler_params=pltpu.CompilerParams(
            collective_id=1, has_side_effects=True, vmem_limit_bytes=60 << 20
        ),
    )(grad_one, grad_two, grad_three, inputs_delta, block_rows, own_small)

    block_out = bo_blocks[:, :rows_here]
    inputs_grad = dx_blocks[:, :rows_here].astype(f32)

    def joined(parts):
        return parts.transpose(1, 0, 2).reshape(per, -1)

    query_weight_grad = joined(sum_one[:, :, :128])
    key_weight_grad = joined(sum_one[:, :, 128:256])
    value_weight_grad = joined(sum_one[:, :, 256:384])
    output_weight_grad = joined(sum_one[:, :, 384:]).T
    up_weight_grad = joined(sum_two)
    down_weight_grad = joined(sum_three).T
    mod_delta = mail[:, 0, :6]
    same = jnp.sum(mail[:, 0, :8], axis=0)
    halves_sum = jnp.sum(mail[:, :, 8:12], axis=0)
    block = f * cs + c

    def mine(values):
        return lax.dynamic_slice_in_dim(values, block * lanes, lanes, values.ndim - 1)

    same = mine(same.reshape(8, heads, HD))
    modulate_bias_grad, output_bias_grad, down_bias_grad = same[:6], same[6], same[7]
    quarter = mine(halves_sum[:, :2].reshape(2, 4, heads // 2, HD)).transpose(1, 0, 2, 3).reshape(4, heads, lanes)
    query_bias_grad, value_bias_grad, query_gain_grad, key_gain_grad = (quarter[j] for j in range(4))
    up_bias_grad = mine(halves_sum[:, 2:].reshape(-1, HD))
    head_max = jnp.max(mail[:, :, 12, :128], axis=0).reshape(heads, HD)[:, 0]

    cond_rows = lax.all_gather(cond_part, "tp", axis=1, tiled=True)
    silu_cond = jax.nn.silu(cond_rows).astype(bf16)
    flat_delta = mod_delta.reshape(every, 6 * width)
    modulate_weight_grad = jnp.einsum(
        "bd,be->de", silu_cond.astype(f32), flat_delta, precision=precise
    ).reshape(per, 6, width)
    silu_delta = jnp.einsum(
        "be,de->bd", flat_delta, modulate_weight.reshape(per, 6 * width).astype(f32), precision=precise
    )
    silu_cols = lax.psum_scatter(silu_delta, "tp", scatter_dimension=1, tiled=True)
    primal, silu_back = jax.vjp(jax.nn.silu, cond_part)
    cond_delta = silu_back(silu_cols)[0]
    class_table_grad = jnp.dot(onehot.astype(f32).T, cond_delta, precision=precise)

    factor = jnp.where(
        head_flags == 1,
        jnp.sqrt(clip_threshold / jnp.maximum(head_max, clip_threshold)),
        jnp.ones_like(head_max),
    )
    columns = jnp.repeat(factor, HD)
    clipped_query = query_weight.astype(f32) * columns[None, :]
    clipped_key = key_weight.astype(f32) * columns[None, :]
    clipped_query_bias = query_bias.astype(f32) * factor[:, None]
    return (
        block_out, inputs_grad, class_table_grad, modulate_weight_grad, modulate_bias_grad,
        query_weight_grad, key_weight_grad, value_weight_grad, query_bias_grad, value_bias_grad,
        query_gain_grad, key_gain_grad, output_weight_grad, output_bias_grad,
        up_weight_grad, up_bias_grad, down_weight_grad, down_bias_grad,
        clipped_query, clipped_key, clipped_query_bias,
    )


def solution(mesh):
    rows = P("fsdp", "ctx", "tp")
    table = P(None, ("fsdp", "ctx", "tp"))
    left = P(("fsdp", "ctx"), "tp")
    right = P("tp", ("fsdp", "ctx"))
    modulate = P(("fsdp", "ctx"), None, "tp")
    modulate_small = P(None, "tp", ("fsdp", "ctx"))
    return jax.shard_map(
        functools.partial(on_device, mesh.shape["fsdp"], mesh.shape["ctx"], mesh.shape["tp"]),
        mesh=mesh,
        in_specs=(
            rows, rows, P(), P(), P("tp"), table, modulate, modulate_small,
            left, left, left, right, right, right, right,
            right, right, left, right, right, right,
        ),
        out_specs=(
            rows, rows, table, modulate, modulate_small,
            left, left, left, right, right, right, right,
            right, right, left, right, right, right,
            left, left, right,
        ),
        check_vma=False,
    )
```

time: 1460 us -> 574 us (0.39)
  waiting for transfers between devices: 831 us -> 5.26 us
  Pallas kernels: 0 us -> 393 us
  blocking collectives: 256 us -> 18.4 us
  matrix products: 208 us -> 54.8 us
  other arithmetic: 67.1 us -> 27.5 us
    reduce_scatter x15 -> x0, waiting for transfers between devices: 591 us -> none  [the longest x2 106 us: branch_sum(): lax.psum_scatter(partial_rows.astype(jnp.bfloat16), 'tp', scatter_dimensi...]
    pallas_call x0 -> x4, Pallas kernels: none -> 393 us  [the longest x1 168 us: on_device(): pl.pallas_call(functools.partial(gather_kernel, fs, cs, ts, padded, per),...]
    all_gather x15 -> x1, blocking collectives: 220 us -> 18.4 us  [on_device(): cond_rows = lax.all_gather(cond_part, 'tp', axis=1, tiled=True)]
    all_gather x9 -> x0, waiting for transfers between devices: 197 us -> none  [the longest x2 119 us: whole_grad(): return lax.all_gather(values, 'tp', axis=2, tiled=True)]
    dot_general x79 -> x15, matrix products: 208 us -> 53.7 us  [the longest x12 51.1 us: product(): return jnp.einsum(form, left, right, preferred_element_type=f32)]
    unnamed x26 -> x2, waiting for transfers between devices: 43.7 us -> 5.25 us
    unnamed x1 -> x0, blocking collectives: 23.2 us -> none
    convert_element_type x24 -> x2, other arithmetic: 23.7 us -> 1.3 us  [the longest x1 1.29 us: on_device(): inputs_grad = dx_blocks[:, :rows_here].astype(f32)]
  transfers between devices with their start and end apart: 25 -> 5, of which waited for: 20 -> 1; matrix products, arithmetic and copies ran while one was open for 15% -> 9% of each run, Pallas kernels for 0% -> 7%
where the time goes in v1:
time: 574 us; the launch traced here: 570 us
  Pallas kernels  393 us (68%)
  matrix products  54.8 us (10%)
  local copies, waits for them, and re-layouts  54.7 us (10%)
  other arithmetic  27.5 us (5%)
  blocking collectives  18.4 us (3%)
  between operations  15.3 us (3%)
    pallas_call x1, Pallas kernels, on_device(): pl.pallas_call(functools.partial(gather_kernel, fs, cs, ts, padded, per),...  168 us
    pallas_call x1, Pallas kernels, on_device(): pl.pallas_call(functools.partial(scatter_kernel, fs, cs, ts, padded, per)...  164 us
    dot_general x12, matrix products, product(): return jnp.einsum(form, left, right, preferred_element_type=f32)  51.1 us
    pallas_call x1, Pallas kernels, on_device(): pl.pallas_call(attention_backward, name='attend_back', grid=(ts,), out_sh...  39.7 us
    unnamed x135, local copies, waits for them, and re-layouts  30.8 us
    pallas_call x1, Pallas kernels, on_device(): pl.pallas_call(attention_forward, name='attend', grid=(ts,), out_shape=(r...  22.1 us
    all_gather x1, blocking collectives, on_device(): cond_rows = lax.all_gather(cond_part, 'tp', axis=1, tiled=True)  18.4 us
  transfers between devices with their start and end apart: 5, of which 1 were waited for; matrix products, arithmetic and copies ran while one was open for 9% of the time, Pallas kernels for 7%

profile of v1, /device:TPU:0, one launch (start us, length us, event | category | flops | bytes accessed | tf_op | source)
XLA Modules:
  0.0 570.1 jit_solution(3747404411910454013)
XLA Ops:
  14.9 1.0 copy.249
  15.8 1.0 copy.243
  18.0 1.1 copy.250
  19.3 1.8 copy.252
  23.9 168.0 %gather.1 = (bf16[704,1024]{1,0:T(8,128)(2,1)S(1)}, bf16[704,1024]{1,0:T(8,128)(2,1)S(1)}, bf16[4,1024,512]{2,1,0:T(8,128)(2,1)S(1)}, bf16[4,1024,512]{2,1,0:T(8...) custom-call(bf16[8,176,256]{2,1,0:T(8,128)(2,1)S(1)} %pad.18.x_ref, ...), custom_call_target="tpu_custom_call" | custom-call | tf_op jit(solution)/shard_map/gather/pallas_call | solution.py:593
  191.9 1.1 copy-done.6
  193.1 1.9 copy-done.13
  195.0 2.1 copy-done.15
  197.1 2.0 copy-done.17
  201.7 1.0 copy.263
  202.7 1.2 reshape.276
  205.5 4.6 fusion.31
  211.6 22.1 %attend.1 = (bf16[704,512]{1,0:T(8,128)(2,1)S(1)}, bf16[704,512]{1,0:T(8,128)(2,1)S(1)}, bf16[704,512]{1,0:T(8,128)(2,1)S(1)}, f32[4,2,704,1]{3,2,1,0:T(8,128)}, f32[4,2,8,128]{3,2,1,0:T(8,128)S(1)}) custom-call(f32[704,512]{1,0:T(8,128)S(1)} %get-tuple-element.224.q_ref, f32[704,512]{1,0:T(8,128)S(1)} %get-tuple-element.223.k_ref, ...), custom_call_target="tpu_custom_call" | custom-call | tf_op jit(solution)/shard_map/attend/pallas_call | solution.py:662
  236.3 3.3 bitcast_convert_fusion.3
  239.6 18.4 %all-gather = f32[4,32,16]{1,2,0:T(8,128)S(1)} all-gather(f32[1,32,16]{1,2,0:T(8,128)S(1)} %bitcast.298), channel_id=1, replica_groups=mesh['fsdp'=2,'ctx'=4,'tp'=4] {'tp'}, dimensions={0}, use_global_device_ids=true | all-gather | bytes 10240 | tf_op jit(solution)/shard_map/all_gather | solution.py:812
  259.3 3.0 convert_reduce_fusion.1
  262.9 3.3 fusion.67
  266.3 4.8 bitcast_convert_fusion
  271.1 6.5 %convert_reduce_fusion = (f32[4,512]{1,0:T(4,128)S(1)}, bf16[4,704,512]{2,1,0:T(8,128)(2,1)S(1)}) fusion(f32[4,512,704]{1,2,0:T(8,128)S(1)} %fusion.67, f32[4,512]{1,0:T(4,128)S(1)} %add.238, bf16[4,1024,512]{2,1,0:T(8,128)(2,1)S(1)} %copy-done.18, f32[1024]{0:T(1024)S(1)} %bitcast.312, bf16[704,1024]{1,0:T(8,128)(2,1)S(1)} %copy-done.7, ...), kind=kOutput, calls=%fused_computation.16 | convolution fusion | flops 2988832768 | bytes 14308032 | tf_op jit(solution)/shard_map/sf,zfh->zsh/dot_general | solution.py:22
  277.6 4.7 bitcast_convert_fusion.2
  282.8 7.9 %convert_bitcast_fusion.1.d2 = bf16[4,1024,512]{2,1,0:T(8,128)(2,1)} fusion(bf16[4,704,512]{2,1,0:T(8,128)(2,1)} %copy-done.54, bf16[704,1024]{1,0:T(8,128)(2,1)} %copy-done.21, f32[1024]{0:T(1024)S(1)} %bitcast.331, f32[1024]{0:T(1024)S(1)} %bitcast.305, f32[704]{0:T(1024)S(1)} %add_rsqrt_fusion, f32[704]{0:T(1024)S(1)} %broadcast_multiply_fusion.4), kind=kOutput, calls=%fused_computation.22 | convolution fusion | flops 2959212544 | bytes 8533504 | tf_op jit(solution)/shard_map/sd,zsh->zdh/dot_general | solution.py:22
  290.8 8.8 %convert_bitcast_fusion.d3 = bf16[4,1024,512]{2,1,0:T(8,128)(2,1)} fusion(bf16[704,1024]{1,0:T(8,128)(2,1)S(1)} %copy-done.7, f32[1024]{0:T(1024)S(1)} %bitcast.313, pred[704]{0:T(1024)(128)(4,1)S(1)} %copy-done.43, f32[4,512,704]{1,2,0:T(8,128)} %copy-done.53, f32[4,512]{1,0:T(4,128)S(1)} %add.238), kind=kOutput, calls=%fused_computation.21 | convolution fusion | flops 2972188672 | bytes 11416256 | tf_op jit(solution)/shard_map/sf,zsh->zfh/dot_general | solution.py:22
  299.5 1.5 fusion.23
  301.1 3.0 convert_reduce_fusion.3
  304.1 1.1 copy-done.28
  306.8 39.7 %attend_back.1 = (bf16[704,512]{1,0:T(8,128)(2,1)S(1)}, bf16[704,512]{1,0:T(8,128)(2,1)S(1)}, bf16[704,512]{1,0:T(8,128)(2,1)S(1)}, f32[4,2,128]{2,1,0:T(2,128)S(1)}) custom-call(f32[704,512]{1,0:T(8,128)} %copy-done.3, f32[704,512]{1,0:T(8,128)} %copy-done.2, bf16[704,512]{1,0:T(8,128)(2,1)S(1)} %copy-done.10, bf16[704,512]{1,0:T(8,128)(2,1)S(1)} %copy-done.12, ...), custom_call_target="tpu_custom_call" | custom-call | tf_op jit(solution)/shard_map/attend_back/pallas_call | solution.py:712
  347.1 2.4 bitcast_convert_fusion.1
  350.0 1.0 fusion.53
  351.1 2.9 convert_bitcast_fusion.2
  354.0 2.4 pad_maximum_fusion.d1
  356.4 4.7 convert_reduce_fusion.2
  361.1 4.3 multiply_reduce_fusion.1
  365.4 1.3 concatenate.20.small_ref
  366.7 163.6 %scatter.1 = (f32[2,128,512]{2,1,0:T(8,128)}, f32[2,128,512]{2,1,0:T(8,128)}, f32[2,128,512]{2,1,0:T(8,128)}, bf16[8,176,256]{2,1,0:T(8,128)(2,1)}, bf16[8,176,2...) custom-call(bf16[4,1024,512]{2,1,0:T(8,128)(2,1)} %pad_maximum_fusion.d1, bf16[4,1024,512]{2,1,0:T(8,128)(2,1)} %convert_bitcast_fusion.1.d2, ...), custom_call_target="tpu_custom_call" | custom-call | tf_op jit(solution)/shard_map/scatter/pallas_call | solution.py:755
  531.2 1.0 slice_reduce_fusion.1
  533.1 1.0 slice.145
  536.9 1.2 convolution_bitcast_fusion
  538.8 1.8 slice_bitcast_fusion.1
  540.7 1.4 fusion.71
  542.1 1.3 slice_convert_fusion
  544.0 1.1 copy.300
  545.8 1.2 copy.298
  547.0 1.0 copy.305
  548.0 1.0 copy.299
  549.0 1.7 copy.297
  550.7 1.0 copy.296
  554.1 1.9 copy.301
  556.0 5.2 reduce-scatter.4.cloned.1.call-done
  (235 shorter events, 35.7 us)
Async XLA Ops:
  7.2 14.9 %copy-start = (bf16[1001,32]{0,1:T(8,128)(2,1)S(1)}, bf16[1001,32]{0,1:T(8,128)(2,1)}, u32[]{:S(2)}) copy-start(bf16[1001,32]{0,1:T(8,128)(2,1)} %param.26) | copy-start | bytes 192196
  7.2 13.9 %copy-start.34 = (bf16[128,6,256]{2,0,1:T(8,128)(2,1)S(1)}, bf16[128,6,256]{2,0,1:T(8,128)(2,1)}, u32[]{:S(2)}) copy-start(bf16[128,6,256]{2,0,1:T(8,128)(2,1)} %param.27) | copy-start | bytes 1179652
  7.2 14.3 %copy-start.31 = (bf16[8,170,256]{2,0,1:T(8,128)(2,1)S(1)}, bf16[8,170,256]{2,0,1:T(8,128)(2,1)}, u32[]{:S(2)}) copy-start(bf16[8,170,256]{2,0,1:T(8,128)(2,1)} %param.21) | copy-start | bytes 2088964
  7.2 14.5 %copy-start.32 = (bf16[8,170,256]{2,0,1:T(8,128)(2,1)S(1)}, bf16[8,170,256]{2,0,1:T(8,128)(2,1)}, u32[]{:S(2)}) copy-start(bf16[8,170,256]{2,0,1:T(8,128)(2,1)} %param.22) | copy-start | bytes 2088964
  7.2 554.0 %reduce-scatter.4.cloned.1.call-start = ((), (), s32[]{:S(2)}) async-start(), calls=%async_computation.1 | async-start | bytes 81920
  7.3 193.7 %copy-start.41 = (pred[704]{0:T(1024)(128)(4,1)}, pred[704]{0:T(1024)(128)(4,1)S(1)}, u32[]{:S(2)}) copy-start(pred[704]{0:T(1024)(128)(4,1)S(1)} %fusion.92) | copy-start | bytes 2116
  193.1 1.9 copy-start.13
  195.0 2.1 copy-start.15
  197.1 2.0 copy-start.17
  201.7 3.9 copy-start.42
  204.6 5.6 copy-start.45
  211.0 28.6 %copy-start.2 = (f32[704,512]{1,0:T(8,128)}, f32[704,512]{1,0:T(8,128)S(1)}, u32[]{:S(2)}) copy-start(f32[704,512]{1,0:T(8,128)S(1)} %get-tuple-element.223.k_ref) | copy-start | bytes 4325380
  211.1 28.6 %copy-start.3 = (f32[704,512]{1,0:T(8,128)}, f32[704,512]{1,0:T(8,128)S(1)}, u32[]{:S(2)}) copy-start(f32[704,512]{1,0:T(8,128)S(1)} %get-tuple-element.224.q_ref) | copy-start | bytes 4325380
  235.4 4.2 copy-start.38
  235.4 23.8 %copy-start.40 = (f32[1,1024]{1,0:T(1,128)S(1)}, f32[1,1024]{1,0:T(1,128)}, u32[]{:S(2)}) copy-start(f32[1,1024]{1,0:T(1,128)} %get-tuple-element.206) | copy-start | bytes 12292
  235.4 23.8 %copy-start.43 = (pred[704]{0:T(1024)(128)(4,1)S(1)}, pred[704]{0:T(1024)(128)(4,1)}, u32[]{:S(2)}) copy-start(pred[704]{0:T(1024)(128)(4,1)} %copy-done.41) | copy-start | bytes 2116
  239.6 19.6 %collective-permute-start = (bf16[704,1024]{1,0:T(8,128)(2,1)}, bf16[704,1024]{1,0:T(8,128)(2,1)}, u32[]{:S(2)}, u32[]{:S(2)}) collective-permute-start(bf16[704,1024]{1,0:T(8,128)(2,1)} %bitcast_convert_fusion.3), channel_id=1, source_target_pairs={{0,4},{4,0},{8,12},{12,8},{1,5},{5,1},{9,13},{13,9},{2,6},{6,2},{1... | collective-permute-start | bytes 4325384 | tf_op jit(solution)/shard_map/ppermute | solution.py:680
  259.3 3.6 copy-start.16
  259.3 3.6 copy-start.39
  259.3 3.6 copy-start.47
  262.3 3.9 copy-start.21
  262.9 3.4 copy-start.18
  266.2 4.8 copy-start.53
  266.2 4.8 copy-start.7
  266.2 4.8 copy-start.44
  277.5 4.7 copy-start.54
  282.3 17.3 %collective-permute-start.1 = (bf16[704,1024]{1,0:T(8,128)(2,1)}, bf16[704,1024]{1,0:T(8,128)(2,1)S(1)}, u32[]{:S(2)}, u32[]{:S(2)}) collective-permute-start(bf16[704,1024]{1,0:T(8,128)(2,1)} %bitcast_convert_fusion.2), channel_id=1, source_target_pairs={{0,4},{4,0},{8,12},{12,8},{1,5},{5,1},{9,13},{13,9},{2,6},{6,2},{1... | collective-permute-start | bytes 4325384 | tf_op jit(solution)/shard_map/ppermute | solution.py:680
  282.3 74.0 %collective-permute-start.3 = (bf16[704,1024]{1,0:T(8,128)(2,1)}, bf16[704,1024]{1,0:T(8,128)(2,1)S(1)}, u32[]{:S(2)}, u32[]{:S(2)}) collective-permute-start(bf16[704,1024]{1,0:T(8,128)(2,1)} %bitcast_convert_fusion), channel_id=1, source_target_pairs={{0,4},{4,0},{8,12},{12,8},{1,5},{5,1},{9,13},{13,9},{2,6},{6,2},{1... | collective-permute-start | bytes 4325384 | tf_op jit(solution)/shard_map/ppermute | solution.py:680
  290.8 8.8 %copy-start.22 = (bf16[704,1024]{1,0:T(8,128)(2,1)S(1)}, bf16[704,1024]{1,0:T(8,128)(2,1)}, u32[]{:S(2)}) copy-start(bf16[704,1024]{1,0:T(8,128)(2,1)} %copy-done.21) | copy-start | bytes 4325380
  290.8 8.8 %copy-start.24 = (bf16[704,1024]{1,0:T(8,128)(2,1)S(1)}, bf16[704,1024]{1,0:T(8,128)(2,1)}, u32[]{:S(2)}) copy-start(bf16[704,1024]{1,0:T(8,128)(2,1)} %bitcast_convert_fusion.2) | copy-start | bytes 4325380
  301.1 4.1 copy-start.14
  305.2 1.3 copy-start.10
  305.2 1.5 copy-start.12
  347.1 2.9 copy-start.20
  347.1 2.9 copy-start.29
  349.5 6.8 %collective-permute-start.2 = (bf16[704,1024]{1,0:T(8,128)(2,1)S(1)}, bf16[704,1024]{1,0:T(8,128)(2,1)S(1)}, u32[]{:S(2)}, u32[]{:S(2)}) collective-permute-start(bf16[704,1024]{1,0:T(8,128)(2,1)S(1)} %bitcast_convert_fusion.1), channel_id=1, source_target_pairs={{0,4},{4,0},{8,12},{12,8},{1,5},{5,1},{9,13},{13,9},{2,6},{6,2},{1... | collective-permute-start | bytes 4325384 | tf_op jit(solution)/shard_map/ppermute | solution.py:680
  349.8 1.2 copy-start.46
  354.0 2.4 copy-start.27
  356.4 4.7 copy-start.23
  366.7 167.7 %copy-start.52 = (s32[4]{0:T(128)S(1)}, s32[4]{0:T(128)}, u32[]{:S(2)}) copy-start(s32[4]{0:T(128)} %param.25) | copy-start | bytes 52
  366.7 167.7 %copy-start.48 = (bf16[4,8]{1,0:T(4,128)(2,1)S(1)}, bf16[4,8]{1,0:T(4,128)(2,1)}, u32[]{:S(2)}) copy-start(bf16[4,8]{1,0:T(4,128)(2,1)} %param.32) | copy-start | bytes 196
  366.7 170.2 %copy-start.26 = (bf16[128,6,256]{0,2,1:T(8,128)(2,1)S(1)}, bf16[128,6,256]{0,2,1:T(8,128)(2,1)}, u32[]{:S(2)}) copy-start(bf16[128,6,256]{0,2,1:T(8,128)(2,1)} %copy-done.25) | copy-start | bytes 1179652
  366.7 171.4 %copy-start.35 = (bf16[128,256]{1,0:T(8,128)(2,1)S(1)}, bf16[128,256]{1,0:T(8,128)(2,1)}, u32[]{:S(2)}) copy-start(bf16[128,256]{1,0:T(8,128)(2,1)} %param.30) | copy-start | bytes 196612
  366.7 171.4 %copy-start.36 = (bf16[128,256]{1,0:T(8,128)(2,1)S(1)}, bf16[128,256]{1,0:T(8,128)(2,1)}, u32[]{:S(2)}) copy-start(bf16[128,256]{1,0:T(8,128)(2,1)} %param.29) | copy-start | bytes 196612
  533.1 10.9 %copy-start.30 = (bf16[8,176,256]{2,1,0:T(8,128)(2,1)S(1)}, bf16[8,176,256]{2,1,0:T(8,128)(2,1)}, u32[]{:S(2)}) copy-start(bf16[8,176,256]{2,1,0:T(8,128)(2,1)} %get-tuple-element.57) | copy-start | bytes 2162692
  542.1 5.9 %copy-start.33 = (f32[2,128,512]{2,1,0:T(8,128)S(1)}, f32[2,128,512]{2,1,0:T(8,128)}, u32[]{:S(2)}) copy-start(f32[2,128,512]{2,1,0:T(8,128)} %get-tuple-element.62) | copy-start | bytes 1572868
  548.0 14.1 %copy-start.51 = (s32[16]{0:T(128)S(1)}, s32[16]{0:T(128)}, u32[]{:S(2)}) copy-start(s32[16]{0:T(128)} %param.23) | copy-start | bytes 196
  548.0 15.0 %copy-start.1 = (bf16[1001,32]{0,1:T(8,128)(2,1)S(1)}, bf16[1001,32]{0,1:T(8,128)(2,1)}, u32[]{:S(2)}) copy-start(bf16[1001,32]{0,1:T(8,128)(2,1)} %param.26) | copy-start | bytes 192196
  (12 other events, 10.9 us)
Sparse Core Ops, SparseCore 0:
  538.2 23.0 reduce-scatter.3
